TPU v7x, 512 devices: a whole 4x4x16 slice. The times are simulated.
512 devices in a mesh: row: 64 (over x, y, z_hi, core), col: 8 (over z_lo).
Axes of the slice: x: 4, y: 4, z: 16 (z_hi: 2, z_lo: 8; z = z_hi * 8 + z_lo), core: 2. Of those that a mesh axis runs over, the one named last changes fastest.
Arguments:
- inputs: bfloat16 [256, 1024, 256], P('row', 'col'), may hold values from -6 to 6
- preactivation: bfloat16 [256, 1024, 256], P('row', 'col'), may hold values from -6 to 6
- cotangent: bfloat16 [256, 1024, 256], P('row', 'col'), may hold values from -6 to 6
- spectral: bfloat16 [2, 128, 64, 5, 1024], P(None, 'row', 'col'), may hold values from -2 to 2
- bypass: bfloat16 [32, 32], replicated, may hold values from -1 to 1
Outputs:
- grad_inputs: bfloat16 [256, 1024, 256], P('row', 'col')
- grad_spectral: float32 [2, 128, 64, 5, 1024], P(None, 'row', 'col')
- grad_bypass: float32 [32, 32], replicated
All inputs are finite; a program needn't handle non-finite values.
Results may differ from a plain program's by a relative error of at most 0.022.
Values may be sent and summed in bfloat16 or wider, within the bound.
A program may use at most 64 MiB of HBM per device.

v0:
```python
import math

import jax
import jax.numpy as jnp
from jax import lax
from jax.sharding import PartitionSpec as P

exact_mode = lax.Precision.HIGHEST


def counting(length):
    return jnp.arange(length, dtype=jnp.int32)


def kept_freq(slot_index, keep_count):
    return jnp.where(slot_index < keep_count // 2, slot_index, slot_index - keep_count)


def phase_table(outer_index, inner_index, length, direction):
    turn_count = jnp.mod(outer_index[:, None] * inner_index[None, :], length)
    angles = turn_count.astype(jnp.float32) * (2.0 * math.pi / length)
    cosine = jnp.cos(angles)
    sine_part = direction * jnp.sin(angles)
    top_rows = jnp.stack([cosine, -sine_part], axis=1)
    low_rows = jnp.stack([sine_part, cosine], axis=1)
    return jnp.stack([top_rows, low_rows], axis=0)


def time_forward(step_count, time_modes):
    turn_count = jnp.mod(counting(step_count)[:, None] * counting(time_modes)[None, :], step_count)
    angles = turn_count.astype(jnp.float32) * (2.0 * math.pi / step_count)
    return jnp.stack([jnp.cos(angles), -jnp.sin(angles)], axis=1)


def time_inverse(step_count, time_modes):
    turn_count = jnp.mod(counting(time_modes)[:, None] * counting(step_count)[None, :], step_count)
    angles = turn_count.astype(jnp.float32) * (2.0 * math.pi / step_count)
    return jnp.stack([jnp.cos(angles), -jnp.sin(angles)], axis=0)


def gelu_slope(values):
    normal_cdf = 0.5 * (1.0 + lax.erf(values * (1.0 / math.sqrt(2.0))))
    density = jnp.exp(-0.5 * values * values) * (1.0 / math.sqrt(2.0 * math.pi))
    return normal_cdf + values * density


def mix_modes(modes_in, modes_grad, weight, factor):
    in_real = modes_in[:, 0]
    in_imag = modes_in[:, 1]
    grad_real = modes_grad[:, 0]
    grad_imag = modes_grad[:, 1]
    real_part = factor * (
        in_real[..., :, None] * grad_real[..., None, :]
        + in_imag[..., :, None] * grad_imag[..., None, :]
    )
    imag_part = factor * (
        in_real[..., :, None] * grad_imag[..., None, :]
        - in_imag[..., :, None] * grad_real[..., None, :]
    )
    weight_grad = jnp.stack([real_part, imag_part], axis=0)
    w_real = weight[0]
    w_imag = weight[1]
    back_real = factor * (
        jnp.einsum("kyscd,kysd->kysc", w_real, grad_real, precision=exact_mode)
        + jnp.einsum("kyscd,kysd->kysc", w_imag, grad_imag, precision=exact_mode)
    )
    back_imag = factor * (
        jnp.einsum("kyscd,kysd->kysc", w_real, grad_imag, precision=exact_mode)
        - jnp.einsum("kyscd,kysd->kysc", w_imag, grad_real, precision=exact_mode)
    )
    return (weight_grad, jnp.stack([back_real, back_imag], axis=1))


def local(inputs, preactivation, cotangent, spectral, bypass):
    row_count, col_count, packed = inputs.shape
    chan_count = bypass.shape[0]
    step_count = packed // chan_count
    time_modes = spectral.shape[3]
    owned_row_modes = spectral.shape[1]
    owned_col_modes = spectral.shape[2]
    row_parts = lax.axis_size("row")
    col_parts = lax.axis_size("col")
    row_modes = owned_row_modes * row_parts
    col_modes = owned_col_modes * col_parts
    total_x = row_count * row_parts
    total_y = col_count * col_parts
    factor = 1.0 / math.sqrt(
        float(total_x * total_y * step_count * row_modes * col_modes * time_modes)
    )
    row_start = lax.axis_index("row") * row_count
    col_start = lax.axis_index("col") * col_count
    mode_width = owned_col_modes * time_modes * chan_count
    slopes = gelu_slope(preactivation.astype(jnp.float32))
    pre_grad = (cotangent.astype(jnp.float32) * slopes).astype(jnp.bfloat16)
    flat_inputs = inputs.reshape(-1, chan_count)
    flat_grad = pre_grad.reshape(-1, chan_count)
    local_bypass = jnp.einsum(
        "nc,nd->cd", flat_inputs, flat_grad, preferred_element_type=jnp.float32
    )
    bypass_total = lax.psum(local_bypass, ("row", "col"))
    grad_bypass = bypass_total * (1.0 / math.sqrt(float(total_x * total_y * step_count)))
    forward_t = time_forward(step_count, time_modes)
    col_table = phase_table(counting(col_modes), col_start + counting(col_count), total_y, -1.0)

    def column_terms(field):
        cube_view = field.astype(jnp.float32).reshape(row_count, col_count, step_count, chan_count)
        in_time = jnp.einsum("rytc,tqs->ryqsc", cube_view, forward_t, precision=exact_mode)
        return jnp.einsum("akpy,rypsc->raksc", col_table, in_time, precision=exact_mode)

    col_in, col_grad = (
        lax.psum_scatter(
            column_terms(inputs).astype(jnp.bfloat16), "col", scatter_dimension=2, tiled=True
        ).astype(jnp.float32),
        lax.psum_scatter(
            column_terms(pre_grad).astype(jnp.bfloat16), "col", scatter_dimension=2, tiled=True
        ).astype(jnp.float32),
    )
    flat_in = col_in.reshape(row_count, 2, mode_width)
    flat_cols = col_grad.reshape(row_count, 2, mode_width)
    stacked = jnp.stack([flat_in, flat_cols], axis=2)
    frequencies = kept_freq(counting(owned_row_modes * lax.axis_size("row")), row_modes)
    phases = phase_table(frequencies, row_start + counting(row_count), total_x, -1.0)
    owned_modes = lax.psum_scatter(
        jnp.einsum("akpr,rpbm->kabm", phases, stacked, precision=exact_mode),
        "row",
        scatter_dimension=0,
        tiled=True,
    )
    modes_in = owned_modes[:, :, 0]
    modes_grad = owned_modes[:, :, 1]
    mode_shape = (owned_row_modes, 2, owned_col_modes, time_modes, chan_count)
    weight = spectral.astype(jnp.float32).reshape(
        2, owned_row_modes, owned_col_modes, time_modes, chan_count, chan_count
    )
    weight_grad, back_modes = mix_modes(
        modes_in.reshape(mode_shape), modes_grad.reshape(mode_shape), weight, factor
    )
    grad_spectral = weight_grad.reshape(spectral.shape)
    flat_back = back_modes.reshape(owned_row_modes, 2, mode_width)
    mode_piece = lax.all_gather(flat_back, "row", axis=0, tiled=True)
    span_count = mode_piece.shape[0]
    frequencies = kept_freq(counting(span_count), row_modes)
    phases = phase_table(row_start + counting(row_count), frequencies, total_x, 1.0)
    rows_back = jnp.einsum("axpk,kpm->xam", phases, mode_piece, precision=exact_mode)
    rows_view = rows_back.reshape(row_count, 2, owned_col_modes, time_modes, chan_count)
    col_piece = lax.all_gather(rows_view.astype(jnp.bfloat16), "col", axis=2, tiled=True).astype(
        jnp.float32
    )
    span_count = col_piece.shape[2]
    phases = phase_table(col_start + counting(col_count), counting(span_count), total_y, 1.0)
    cells_y = jnp.zeros(
        (row_count, col_count, 2, time_modes, chan_count), jnp.float32
    ) + jnp.einsum("aypk,rpksc->ryasc", phases, col_piece, precision=exact_mode)
    kernel_grad = jnp.einsum(
        "ryasc,ast->rytc", cells_y, time_inverse(step_count, time_modes), precision=exact_mode
    )
    bypass_grad = jnp.einsum("nd,cd->nc", flat_grad, bypass, preferred_element_type=jnp.float32)
    total_grad = kernel_grad.reshape(-1, chan_count) + bypass_grad
    grad_inputs = total_grad.reshape(inputs.shape).astype(jnp.bfloat16)
    return (grad_inputs, grad_spectral, grad_bypass)


def solution(mesh):
    return jax.shard_map(
        local,
        mesh=mesh,
        in_specs=(
            P("row", "col", None),
            P("row", "col", None),
            P("row", "col", None),
            P(None, "row", "col", None, None),
            P(),
        ),
        out_specs=(P("row", "col", None), P(None, "row", "col", None, None), P()),
        check_vma=False,
    )
```

profile of v0, /device:TPU:1, one launch (start us, length us, event | category | flops | bytes accessed | tf_op | source)
XLA Modules:
  0.0 1425.6 jit_solution(1506078009365955725)
XLA Ops:
  7.2 0.0 all-reduce.9.cloned.1.call-start
  7.2 0.1 sine_negate_fusion
  7.3 0.1 fusion.55
  7.5 1.1 copy.63
  8.6 1.1 copy.64
  9.7 0.3 fusion.28
  10.0 0.6 convolution_bitcast_fusion.2
  10.6 0.7 fusion.7
  11.3 1.2 copy.67
  12.5 0.2 copy.58
  12.6 0.6 convolution_bitcast_fusion.3
  13.2 0.7 fusion.8
  14.0 1.2 copy.61
  15.1 0.0 all-reduce.9.cloned.1.call-update
  15.2 0.0 all-reduce.7.cloned.1.call-start
  15.3 1.3 dynamic-slice
  17.2 0.1 fusion.100
  17.3 128.2 %all-reduce.9.cloned.1.call-done = (bf16[4,2,64,5,32]{4,0,3,1,2:T(4,128)(2,1)}, bf16[4,2,64,5,32]{4,0,3,1,2:T(4,128)(2,1)}) async-done(((bf16[4,2,64,5,32]{4,0,3,1,2:T(4,128)(2,1)}, bf16[4,2,64,5,32]{4,0,3,1,2:T(4,128)(2,1)}), (bf16[4,2,64,5,32]{4,0,3,1,2:T(4,128)(2,1)}, bf16[4,2,64,5,32]{4,0,3,1,2:T(4,128)(2,1)})) %all-reduce.9.cloned.1.call-update) | async-done | bytes 327696
  145.5 0.9 constant_dynamic-slice_fusion.1
  146.4 0.1 reshape.907
  146.6 0.9 constant_dynamic-slice_fusion
  147.5 0.1 reshape.908
  147.7 1.2 convolution_bitcast_fusion
  148.9 3.3 copy.71
  152.2 0.0 all-reduce.7.cloned.1.call-update
  152.3 0.0 all-gather.2.cloned.1.call-start
  152.3 1.3 dynamic-slice.4
  153.6 0.4 squeeze.13
  154.1 0.4 squeeze.15
  155.2 1085.9 %all-reduce.7.cloned.1.call-done = f32[128,2,2,1280]{3,2,1,0:T(2,128)} async-done(((f32[128,2,2,1280]{3,2,1,0:T(2,128)}), f32[128,2,2,1280]{3,2,1,0:T(2,128)}) %all-reduce.7.cloned.1.call-update) | async-done | bytes 2621456
  1241.1 1.0 dynamic-slice_reduce_fusion
  1242.0 0.1 reshape_squeeze.6
  1242.2 1.1 fusion.19
  1243.3 1.1 fusion.17
  1244.4 1.1 fusion.15
  1245.6 1.1 fusion.13
  1246.7 0.1 stack.120
  1246.8 0.1 stack.121
  1247.0 0.6 copy.72
  1247.6 0.0 all-gather.2.cloned.1.call-update
  1247.6 0.1 copy.78
  1247.8 0.4 reshape.882
  1248.2 0.4 reshape.881
  1248.7 0.4 convolution_bitcast_fusion.8
  1249.1 111.3 %psum.7 = f32[32,32]{0,1:T(8,128)S(1)} all-reduce(f32[32,32]{0,1:T(8,128)S(1)} %convolution_bitcast_fusion.8), channel_id=1, replica_groups=mesh['row'=64,'col'=8] {'row','col'}, use_global_device_ids=true, to_apply=%region_3.4 | all-reduce | flops 1024 | bytes 8192 | tf_op jit(solution)/shard_map/psum | solution.py:100
  1360.4 0.7 copy.85
  1361.1 0.1 sine_negate_fusion.1
  1361.1 0.1 fusion.99
  1361.3 0.1 fusion.54
  1361.5 0.1 reshape_squeeze.7
  1361.6 1.7 add_multiply_fusion
  1363.3 1.9 mul.549
  1365.2 0.6 mul.553
  1365.9 0.9 pad_maximum_fusion
  1366.7 2.1 fusion.2
  1368.8 0.2 reshape.909
  1369.0 40.9 %all_gather.7 = bf16[4,2,64,5,32]{4,2,1,3,0:T(8,128)(2,1)S(1)} all-gather(bf16[4,2,8,5,32]{4,2,1,3,0:T(8,128)(2,1)S(1)} %copy.75), channel_id=1, replica_groups=mesh['row'=64,'col'=8] {'col'}, dimensions={2}, use_global_device_ids=true | all-gather | bytes 184320 | tf_op jit(solution)/shard_map/all_gather | solution.py:146
  1409.9 0.7 convolution_bitcast_fusion.4
  1410.6 1.8 convolution_bitcast_fusion.7
  1412.5 1.7 copy.77
  1414.2 1.4 copy.79
  1415.6 1.5 fusion
  1417.1 0.5 copy.80
  1417.6 1.4 convert_element_type.163
  (28 shorter events, 0.3 us)
Async XLA Ops:
  7.2 1408.5 %copy-start = (bf16[32,32]{1,0:T(8,128)(2,1)S(1)}, bf16[32,32]{1,0:T(8,128)(2,1)}, u32[]{:S(2)}) copy-start(bf16[32,32]{1,0:T(8,128)(2,1)} %param.9) | copy-start | bytes 6148
  7.2 138.3 %all-reduce.9.cloned.1.call-start = ((), (), s32[]{:S(2)}) async-start(), calls=%async_computation.2 | async-start | bytes 2621440
  10.6 1.9 copy-start.1
  15.2 1225.9 %all-reduce.7.cloned.1.call-start = ((), (), s32[]{:S(2)}) async-start(), calls=%async_computation.1 | async-start | bytes 5242880
  152.2 1.4 copy-start.2
  152.3 1214.5 %all-gather.2.cloned.1.call-start = ((), (), s32[]{:S(2)}) async-start(), calls=%async_computation | async-start | bytes 1331200 | tf_op jit(solution)/shard_map/all_gather | solution.py:140
Sparse Core Ops, SparseCore 0:
  15.3 130.1 all-reduce.8
  152.4 1088.6 all-reduce.6
  1247.7 107.1 all-gather.1
where the time goes:
time: 1430 us
  waiting for transfers between devices  1210 us (85%)
  blocking collectives  152 us (11%)
  local copies, waits for them, and re-layouts  25.2 us (2%)
  between operations  15.4 us (1%)
  matrix products  14.9 us (1%)
    unnamed x5, waiting for transfers between devices  1210 us
    psum x1, blocking collectives, local(): bypass_total = lax.psum(local_bypass, ('row', 'col'))  111 us
    all_gather x1, blocking collectives, local(): lax.all_gather(rows_view.astype(jnp.bfloat16), 'col', axis=2, tiled=True)  40.9 us
  transfers between devices with their start and end apart: 3, of which 2 were waited for; matrix products, arithmetic and copies ran while one was open for 1% of the time, Pallas kernels for 0%

commit v1 on v0

v1 whole, which is shorter than its diff:
```python
import math

import jax
import jax.numpy as jnp
import numpy as np
from jax import lax
from jax.experimental import pallas as pl
from jax.experimental.pallas import tpu as pltpu
from jax.sharding import PartitionSpec as P

MESH = pl.DeviceIdType.MESH
F32 = jnp.float32
BF16 = jnp.bfloat16
NX, NY, NT, C = 256, 1024, 8, 32
KX, KY, KT = 128, 64, 5
FACTOR = 1.0 / math.sqrt(float(NX * NY * NT * KX * KY * KT))
BYPASS_SCALE = 1.0 / math.sqrt(float(NX * NY * NT))


def turns(a, b, n):
    angle = 2.0 * np.pi * (np.multiply.outer(a, b) % n) / n
    return np.cos(angle), np.sin(angle)


def column_tables():
    forward, inverse = [], []
    for j in range(8):
        cos, sin = turns(np.arange(64), 128 * j + np.arange(128), NY)
        forward.append(np.concatenate([cos, -sin], 0))
        inverse.append(np.concatenate([cos.T, -sin.T], 1))
    return np.stack(forward), np.stack(inverse)


def time_tables():
    cos, sin = turns(np.arange(NT), np.arange(KT), NT)
    eye = np.eye(C)
    low = np.zeros((2, NT, C, 2, 4, C))
    for t in range(NT):
        for k in range(4):
            low[0, t, :, 0, k, :] = eye * cos[t, k]
            low[1, t, :, 0, k, :] = eye * sin[t, k]
            low[0, t, :, 1, k, :] = -eye * sin[t, k]
            low[1, t, :, 1, k, :] = eye * cos[t, k]
    high = np.zeros((2, 2, NT, C, 2, 2, C))
    for f in range(2):
        for t in range(NT):
            high[f, 0, t, :, f, 0, :] = eye * cos[t, 4]
            high[f, 1, t, :, f, 1, :] = eye * cos[t, 4]
    forward = np.stack(
        [
            np.concatenate([low.reshape(512, 256), high[f].reshape(512, 128)], 1)
            for f in range(2)
        ]
    )
    inverse = np.zeros((3, 4, C, 2, NT, C))
    for t in range(NT):
        for k in range(4):
            inverse[0, k, :, 0, t, :] = eye * cos[t, k]
            inverse[1, k, :, 0, t, :] = -eye * sin[t, k]
            inverse[0, k, :, 1, t, :] = eye * sin[t, k]
            inverse[1, k, :, 1, t, :] = eye * cos[t, k]
        inverse[2, 0, :, 0, t, :] = eye * cos[t, 4]
        inverse[2, 1, :, 1, t, :] = eye * cos[t, 4]
    return forward, inverse.reshape(384, 512)


def regroup_tables():
    direct = np.zeros((8, 3, 2, 4, 5, 4, 8))
    swapped = np.zeros((8, 3, 2, 4, 5, 4, 8))
    back = np.zeros((4, 3, 8, 8, 2, 2, 4))
    for k in range(8):
        for x in range(4):
            for tile in range(5):
                direct[k, tile // 2, tile % 2, x, tile, x, k] = 1.0
            swapped[k, 2, 1, x, 4, x, k] = 1.0
            for tile in range(3):
                back[x, tile, k, k, tile // 2, tile % 2, x] = 1.0
    lanes = np.zeros((2, 2, C, 2, 2, C))
    for f in range(2):
        lanes[f, 1, :, f, 0, :] = np.eye(C)
        lanes[f, 0, :, f, 1, :] = -np.eye(C)
    return (
        direct.reshape(192, 160),
        swapped.reshape(192, 160),
        lanes.reshape(128, 128),
        back.reshape(96, 128),
    )


def row_tables():
    k = np.arange(KX)
    freq = np.where(k < KX // 2, k, k - KX) % NX
    cos, sin = turns(freq, np.arange(NX), NX)
    cos = cos.reshape(4, 16, 2, 4, 4, 2, 2, 4)
    sin = sin.reshape(4, 16, 2, 4, 4, 2, 2, 4)
    forward = np.zeros((4, 4, 16, 2, 2, 2, 2, 2, 4, 2, 2, 4))
    for xx in range(4):
        for slab in range(2):
            c = cos[:, :, :, xx].transpose(0, 1, 2, 4, 3, 5, 6)
            s = sin[:, :, :, xx].transpose(0, 1, 2, 4, 3, 5, 6)
            forward[xx, :, :, slab, :, 0, slab, :, :, :, 0, :] = c
            forward[xx, :, :, slab, :, 0, slab, :, :, :, 1, :] = s
            forward[xx, :, :, slab, :, 1, slab, :, :, :, 1, :] = c
            forward[xx, :, :, slab, :, 1, slab, :, :, :, 0, :] = -s
    forward = forward.reshape(4, 512, 256)
    inverse = np.zeros((4, 2, 4, 2, 2, 2, 4, 4, 16, 2, 2, 2))
    for xx in range(4):
        for zh in range(2):
            for slab in range(2):
                c = cos[:, :, :, xx, :, zh].transpose(3, 4, 5, 0, 1, 2)
                s = sin[:, :, :, xx, :, zh].transpose(3, 4, 5, 0, 1, 2)
                inverse[xx, zh, :, :, slab, 0, :, :, :, slab, :, 0] = c
                inverse[xx, zh, :, :, slab, 0, :, :, :, slab, :, 1] = -s
                inverse[xx, zh, :, :, slab, 1, :, :, :, slab, :, 1] = c
                inverse[xx, zh, :, :, slab, 1, :, :, :, slab, :, 0] = s
    return forward, inverse.reshape(8, 128, 512)


def mixing_tables():
    pick = np.zeros((2, 2, 2, 5, 8, 16, 2, 2, 2))
    pick_mask = np.zeros((2, 2, 2, 5, 8, 4, C))
    spread = np.zeros((8, 2, 2, 2, 4, 2, 5, 8))
    spread_mask = np.zeros((4, 2, 5, 8, 4, C))
    for ky in range(8):
        for e in range(2):
            for f in range(2):
                source = (ky // 2) * 4 + f * 2 + ky % 2
                for ri in range(2):
                    for kt in range(4):
                        pick[f, ri, e, kt, ky, source, 0, e, ri] = 1.0
                        pick_mask[f, ri, e, kt, ky, kt, :] = 1.0
                    pick[f, ri, e, 4, ky, source, 1, e, 0] = 1.0
                    pick_mask[f, ri, e, 4, ky, f * 2 + ri, :] = 1.0
            for kt in range(4):
                spread_mask[0, e, kt, ky, kt] = 1.0
                spread_mask[1, e, kt, ky, kt] = 1.0
                spread[ky, 0, e, 0, 0, e, kt, ky] = 1.0
                spread[ky, 0, e, 1, 1, e, kt, ky] = 1.0
            spread_mask[0, e, 4, ky, 0] = 1.0
            spread_mask[1, e, 4, ky, 1] = 1.0
            spread_mask[2, e, 4, ky, 0] = 1.0
            spread_mask[3, e, 4, ky, 1] = 1.0
            spread[ky, 1, e, 0, 0, e, 4, ky] = 1.0
            spread[ky, 1, e, 0, 1, e, 4, ky] = 1.0
            spread[ky, 1, e, 1, 2, e, 4, ky] = 1.0
            spread[ky, 1, e, 1, 3, e, 4, ky] = -1.0
    group = np.arange(128) % C
    lane = np.arange(C * C)
    by_in = (group[:, None] == lane[None, :] // C).astype(np.float64)
    by_out = (group[:, None] == lane[None, :] % C).astype(np.float64)
    return (
        pick.reshape(320, 128),
        pick_mask.reshape(320, 128),
        by_in,
        by_out,
        by_in.T,
        spread.reshape(64, 320),
        spread_mask.reshape(320, 128),
    )


def make_tables():
    t = {}
    t["col_f"], t["col_i"] = column_tables()
    t["time_f"], t["time_i"] = time_tables()
    t["reg_a"], t["reg_b"], t["reg_l"], t["reg_c"] = regroup_tables()
    t["row_f"], t["row_i"] = row_tables()
    t["pick"], t["pick_m"], t["by_in"], t["by_out"], t["by_in_t"], t["spread"], t["spread_m"] = (
        mixing_tables()
    )
    t["rep"] = (np.arange(256)[:, None] % C == np.arange(128)[None, :] % C).astype(np.float64)
    return {k: np.asarray(v, np.float32).astype(jnp.bfloat16) for k, v in t.items()}


PICKED = ("col_f", "col_i", "row_f", "row_i")
ORDER = (
    "col_f", "time_f", "rep", "reg_a", "reg_b", "reg_l", "row_f", "pick", "pick_m", "by_in",
    "by_out", "by_in_t", "spread", "spread_m", "row_i", "reg_c", "time_i", "col_i",
)


def mm(a, b):
    return jnp.dot(a, b, preferred_element_type=F32)


def mm_full(a, b):
    return jnp.dot(a, b, preferred_element_type=F32, precision=lax.Precision.HIGHEST)


def gelu_slope(values):
    normal_cdf = 0.5 * (1.0 + lax.erf(values * (1.0 / math.sqrt(2.0))))
    density = jnp.exp(-0.5 * values * values) * (1.0 / math.sqrt(2.0 * math.pi))
    return normal_cdf + values * density


def pre_gradient(cot, pre):
    return (cot.astype(F32) * gelu_slope(pre.astype(F32))).astype(BF16)


def column_time(field, col_f, time_f):
    y = mm(col_f, field).astype(BF16)
    return mm(jnp.concatenate([y[:64], y[64:]], axis=1), time_f)


def group_mask(shape):
    row = lax.broadcasted_iota(jnp.int32, shape, 0)
    lane = lax.broadcasted_iota(jnp.int32, shape, 1)
    return row, lane


def pack_bypass(product, rep):
    row, lane = group_mask((256, 256))
    kept = jnp.where(row // C == lane // C, product, 0.0)
    wide = mm_full(kept, rep.astype(F32))
    wide = wide.reshape(8, C, 128).sum(0)
    row, lane = group_mask((C, 128))
    kept = jnp.where(row % 4 == lane // C, wide, 0.0)
    row, lane = group_mask((8, C))
    return mm_full(jnp.where(row == lane // 4, 1.0, 0.0), kept)


def unpack_bypass(packed):
    row, lane = group_mask((C, 8))
    wide = mm_full(jnp.where(row // 4 == lane, 1.0, 0.0), packed)
    row, lane = group_mask((C, 128))
    kept = jnp.where(row % 4 == lane // C, wide, 0.0)
    row, lane = group_mask((128, C))
    return mm_full(kept, jnp.where(row % C == lane, 1.0, 0.0)) * BYPASS_SCALE


def block_bypass(bypass):
    row, lane = group_mask((256, C))
    tall = jnp.where(row % C == lane, 1.0, 0.0).astype(BF16)
    row, lane = group_mask((C, 256))
    flat = jnp.where(lane % C == row, 1.0, 0.0).astype(BF16)
    turned = lax.dot_general(tall, bypass, (((1,), (1,)), ((), ())), preferred_element_type=F32)
    full = mm(turned.astype(BF16), flat)
    row, lane = group_mask((256, 256))
    return jnp.where(row // C == lane // C, full, 0.0).astype(BF16)


def regroup_forward(total, reg_a, reg_b, reg_l):
    rows = total.astype(BF16)
    turned = mm(rows, reg_l).astype(BF16)
    return mm(reg_a, rows) + mm(reg_b, turned)


def mixing(modes, w_re, w_im, pick, pick_m, by_in, by_out, by_in_t, spread, spread_m):
    chosen = (mm(pick, modes) * pick_m.astype(F32)).astype(BF16)
    a = mm(chosen[:160], by_in)
    g = mm(chosen[160:], by_out)
    a_re, a_im, g_re, g_im = a[:80], a[80:], g[:80], g[80:]
    out_re = FACTOR * (a_re * g_re + a_im * g_im)
    out_im = FACTOR * (a_re * g_im - a_im * g_re)
    p_re = w_re * g_re + w_im * g_im
    p_im = w_re * g_im - w_im * g_re
    b_re = mm(p_re.astype(BF16), by_in_t) * FACTOR
    b_im = mm(p_im.astype(BF16), by_in_t) * FACTOR
    stack = jnp.concatenate([b_re, b_im, b_im, b_re], axis=0) * spread_m.astype(F32)
    return out_re, out_im, mm(spread, stack.astype(BF16))


def final_rows(low_re, low_im, high, time_i, col_i):
    z = jnp.concatenate([low_re, low_im, high], axis=1)
    u = mm(z, time_i).astype(BF16)
    return mm(col_i, jnp.concatenate([u[:, :256], u[:, 256:]], axis=0))


def rows_of(block, count):
    return block.astype(F32).reshape(count, 128).astype(BF16)


def kernel(inp, pre, cot, spec, byp, *refs):
    n = len(ORDER)
    tables = dict(zip(ORDER, refs[:n]))
    out_g, out_s, out_b = refs[n : n + 3]
    held = dict(zip(ORDER, refs[n + 3 : 2 * n + 3]))
    (
        grad, plus, pieces, recv_col, send_s, recv_s, rows_all, send_x, recv_x, send_q, recv_q,
        send_b, recv_b, recv_g, send_l, recv_l, send_c, recv_c,
        sum_a, sum_b, sum_c, sum_d, by_a, by_b, by_c, by_d,
        table_sem, send_sem, recv_sem,
    ) = refs[2 * n + 3 :]

    row = lax.axis_index("row")
    j = lax.axis_index("col")
    xx = row // 16
    q = row % 16
    yy = q // 4
    zh = (q // 2) % 2
    core = q % 2
    s = yy * 2 + core

    def col_peer(k):
        return row, (j + k) % 8

    def s_index(k):
        return (s + k) % 8

    def s_peer(k):
        other = s_index(k)
        return xx * 16 + (other // 2) * 4 + zh * 2 + other % 2, j

    def zh_peer():
        return xx * 16 + yy * 4 + (1 - zh) * 2 + core, j

    def x_peer(k):
        return ((xx + k) % 4) * 16 + q, j

    def q_index(k):
        return (q + k) % 16

    def q_peer(k):
        return xx * 16 + q_index(k), j

    barrier = pltpu.get_barrier_semaphore()
    everyone = (
        [col_peer(k) for k in range(1, 8)]
        + [q_peer(k) for k in range(1, 16)]
        + [x_peer(k) for k in range(1, 4)]
    )
    for peer in everyone:
        pl.semaphore_signal(barrier, inc=1, device_id=peer, device_id_type=MESH)

    index_of = {"col_f": j, "col_i": j, "row_f": xx, "row_i": xx * 2 + zh}
    loads = {}
    for at, name in enumerate(ORDER):
        source = tables[name].at[index_of[name]] if name in PICKED else tables[name]
        loads[name] = pltpu.make_async_copy(source, held[name], table_sem.at[at])
        loads[name].start()

    def table(name):
        return held[name][...]

    sent = []

    def send(source, target, peer):
        at = len(sent)
        copy = pltpu.make_async_remote_copy(
            src_ref=source,
            dst_ref=target,
            send_sem=send_sem.at[at],
            recv_sem=recv_sem.at[at],
            device_id=peer,
            device_id_type=MESH,
        )
        copy.start()
        sent.append(copy)
        return copy

    def arrive(copies):
        for copy in copies:
            copy.wait_recv()

    loads["col_f"].wait()
    loads["time_f"].wait()
    col_f = table("col_f")
    high = []
    for x in range(4):
        r = column_time(inp[x], col_f, held["time_f"][0])
        pieces[:, 0, x] = r[:, :128].reshape(8, 8, 128).astype(BF16)
        pieces[:, 1, x] = r[:, 128:256].reshape(8, 8, 128).astype(BF16)
        high.append(r[:, 256:])
    pl.semaphore_wait(barrier, len(everyone))
    first = []
    for k in range(1, 8):
        to = (j + k) % 8
        first.append(send(pieces.at[to, 0:2], recv_col.at[k - 1, 0:2], col_peer(k)))
    for x in range(4):
        g = pre_gradient(cot[x], pre[x])
        grad[x] = g
        r = column_time(g, col_f, held["time_f"][1])
        pieces[:, 2, x] = r[:, :128].reshape(8, 8, 128).astype(BF16)
        pieces[:, 3, x] = r[:, 128:256].reshape(8, 8, 128).astype(BF16)
        pieces[:, 4, x] = (high[x] + r[:, 256:]).reshape(8, 8, 128).astype(BF16)
    for k in range(1, 8):
        to = (j + k) % 8
        first.append(send(pieces.at[to, 2:5], recv_col.at[k - 1, 2:5], col_peer(k)))

    product = jnp.zeros((256, 256), F32)
    for x in range(4):
        product += lax.dot_general(
            inp[x], grad[x], (((0,), (0,)), ((), ())), preferred_element_type=F32
        )
    loads["rep"].wait()
    by_a[j] = pack_bypass(product, table("rep"))
    bypass_a = [send(by_a.at[j], by_a.at[j], col_peer(k)) for k in range(1, 8)]
    blocks = block_bypass(byp[...])
    for x in range(4):
        plus[x] = mm(grad[x], blocks)

    for name in ("reg_a", "reg_b", "reg_l"):
        loads[name].wait()
    arrive(first)
    total = pieces[j].astype(F32).reshape(160, 128)
    for k in range(7):
        total += recv_col[k].astype(F32).reshape(160, 128)
    grouped = regroup_forward(total, table("reg_a"), table("reg_b"), table("reg_l"))
    send_s[...] = grouped.reshape(8, 3, 8, 128).astype(BF16)
    recv_s[s] = send_s[s]
    second = [send(send_s.at[s_index(k)], recv_s.at[s], s_peer(k)) for k in range(1, 8)]

    arrive(bypass_a)
    by_b[s] = by_a[...].sum(0)
    bypass_b = [send(by_b.at[s], by_b.at[s], s_peer(k)) for k in range(1, 8)]

    arrive(second)
    rows_all[0, zh] = recv_s[:, zh]
    rows_all[1, zh] = recv_s[:, 2]
    third = [
        send(recv_s.at[:, 1 - zh], rows_all.at[0, zh], zh_peer()),
        send(recv_s.at[:, 2], rows_all.at[1, zh], zh_peer()),
    ]
    arrive(bypass_b)
    by_c[zh] = by_b[...].sum(0)
    bypass_c = [send(by_c.at[zh], by_c.at[zh], zh_peer())]

    loads["row_f"].wait()
    arrive(third)
    partial = mm(table("row_f"), rows_of(rows_all[...], 256))
    send_x[...] = partial.reshape(4, 16, 8, 128).astype(BF16)
    fourth = [
        send(send_x.at[(xx + k) % 4], recv_x.at[k - 1], x_peer(k)) for k in range(1, 4)
    ]
    arrive(bypass_c)
    by_d[xx] = by_c[...].sum(0)
    bypass_d = [send(by_d.at[xx], by_d.at[xx], x_peer(k)) for k in range(1, 4)]
    arrive(fourth)
    summed = send_x[xx].astype(F32)
    for k in range(3):
        summed += recv_x[k].astype(F32)
    send_q[...] = summed.astype(BF16)

    recv_q[q] = send_q[q]
    fifth = [send(send_q.at[q_index(k)], recv_q.at[q], q_peer(k)) for k in range(1, 16)]
    for name in ("pick", "pick_m", "by_in", "by_out", "by_in_t", "spread", "spread_m"):
        loads[name].wait()
    arrive(bypass_d)
    out_b[...] = unpack_bypass(by_d[...].sum(0))
    arrive(fifth)
    out_re, out_im, back = mixing(
        rows_of(recv_q[...], 128),
        spec[0].astype(F32),
        spec[1].astype(F32),
        *[
            table(name)
            for name in ("pick", "pick_m", "by_in", "by_out", "by_in_t", "spread", "spread_m")
        ],
    )
    send_b[...] = back.reshape(8, 8, 128).astype(BF16)
    recv_b[q] = send_b[s]
    sixth = []
    for k in range(1, 16):
        to = q_index(k)
        sixth.append(send(send_b.at[(to // 4) * 2 + to % 2], recv_b.at[q], q_peer(k)))
    out_s[0] = out_re
    out_s[1] = out_im

    arrive(sixth)
    recv_g[xx] = recv_b[...]
    seventh = [send(recv_b, recv_g.at[xx], x_peer(k)) for k in range(1, 4)]
    loads["row_i"].wait()
    loads["reg_c"].wait()
    arrive(seventh)
    lines = mm(table("row_i"), rows_of(recv_g[...], 512))
    send_l[...] = lines.reshape(8, 16, 128).astype(BF16)
    recv_l[s] = send_l[s]
    eighth = [send(send_l.at[s_index(k)], recv_l.at[s], s_peer(k)) for k in range(1, 8)]
    arrive(eighth)
    turned = mm(table("reg_c"), rows_of(recv_l[...], 128))
    send_c[...] = turned.reshape(4, 3, 8, 128).astype(BF16)
    recv_c[j] = send_c[...]
    ninth = [send(send_c, recv_c.at[j], col_peer(k)) for k in range(1, 8)]
    loads["time_i"].wait()
    loads["col_i"].wait()
    time_i = table("time_i")
    col_i = table("col_i")
    arrive(ninth)
    for x in range(4):
        parts = [rows_of(recv_c[:, x, tile], 64) for tile in range(3)]
        out_g[x] = (final_rows(*parts, time_i, col_i) + plus[x]).astype(BF16)

    for copy in sent:
        copy.wait_send()


N_COPIES = 14 + 7 + 7 + 7 + 2 + 1 + 3 + 3 + 15 + 15 + 3 + 7 + 7


def local(inputs, preactivation, cotangent, spectral, bypass, tables):
    weight = spectral.transpose(0, 1, 3, 2, 4).reshape(2, 80, C * C)
    vmem = pl.BlockSpec(memory_space=pltpu.VMEM)
    anywhere = pl.BlockSpec(memory_space=pl.ANY)
    held = [
        pltpu.VMEM(tables[k].shape[1:] if k in PICKED else tables[k].shape, BF16) for k in ORDER
    ]
    blocks = [
        pltpu.VMEM((4, 128, 256), BF16),
        pltpu.VMEM((4, 128, 256), F32),
        pltpu.VMEM((8, 5, 4, 8, 128), BF16),
        pltpu.VMEM((7, 5, 4, 8, 128), BF16),
        pltpu.VMEM((8, 3, 8, 128), BF16),
        pltpu.VMEM((8, 3, 8, 128), BF16),
        pltpu.VMEM((2, 2, 8, 8, 128), BF16),
        pltpu.VMEM((4, 16, 8, 128), BF16),
        pltpu.VMEM((3, 16, 8, 128), BF16),
        pltpu.VMEM((16, 8, 128), BF16),
        pltpu.VMEM((16, 8, 128), BF16),
        pltpu.VMEM((8, 8, 128), BF16),
        pltpu.VMEM((16, 8, 128), BF16),
        pltpu.VMEM((4, 16, 8, 128), BF16),
        pltpu.VMEM((8, 16, 128), BF16),
        pltpu.VMEM((8, 16, 128), BF16),
        pltpu.VMEM((4, 3, 8, 128), BF16),
        pltpu.VMEM((8, 4, 3, 8, 128), BF16),
        pltpu.VMEM((8, 128), F32),
        pltpu.VMEM((8, 128), F32),
        pltpu.VMEM((8, 128), F32),
        pltpu.VMEM((8, 128), F32),
        pltpu.VMEM((8, 8, 128), F32),
        pltpu.VMEM((8, 8, 128), F32),
        pltpu.VMEM((2, 8, 128), F32),
        pltpu.VMEM((4, 8, 128), F32),
        pltpu.SemaphoreType.DMA((len(ORDER),)),
        pltpu.SemaphoreType.DMA((N_COPIES,)),
        pltpu.SemaphoreType.DMA((N_COPIES,)),
    ]
    grad_inputs, grad_weight, grad_bypass = pl.pallas_call(
        kernel,
        out_shape=(
            jax.ShapeDtypeStruct((4, 128, 256), BF16),
            jax.ShapeDtypeStruct((2, 80, C * C), F32),
            jax.ShapeDtypeStruct((C, C), F32),
        ),
        in_specs=[vmem] * 5 + [anywhere] * len(ORDER),
        out_specs=(vmem, vmem, vmem),
        scratch_shapes=held + blocks,
        compiler_params=pltpu.CompilerParams(
            collective_id=0, has_side_effects=True, vmem_limit_bytes=48 * 1024 * 1024
        ),
        name="fno_backward",
    )(inputs, preactivation, cotangent, weight, bypass, *[tables[k] for k in ORDER])
    grad_spectral = grad_weight.reshape(2, 2, 5, 8, C * C).transpose(0, 1, 3, 2, 4)
    return (grad_inputs, grad_spectral, grad_bypass)


def solution(mesh):
    tables = make_tables()

    def step(*args):
        return local(*args, {k: jnp.asarray(v) for k, v in tables.items()})

    return jax.shard_map(
        step,
        mesh=mesh,
        in_specs=(
            P("row", "col", None),
            P("row", "col", None),
            P("row", "col", None),
            P(None, "row", "col", None, None),
            P(),
        ),
        out_specs=(P("row", "col", None), P(None, "row", "col", None, None), P()),
        check_vma=False,
    )
```

time: 1430 us -> 108 us (0.08)
  waiting for transfers between devices: 1210 us -> 0 us
  blocking collectives: 152 us -> 0 us
  Pallas kernels: 0 us -> 84.3 us
  matrix products: 14.9 us -> 0 us
  between operations: 15.4 us -> 0.67 us
    unnamed x5 -> x0, waiting for transfers between devices: 1210 us -> none
    psum x1 -> x0, blocking collectives: 111 us -> none  [local(): bypass_total = lax.psum(local_bypass, ('row', 'col'))]
    pallas_call x0 -> x1, Pallas kernels: none -> 84.3 us  [local(): pl.pallas_call(kernel, out_shape=(jax.ShapeDtypeStruct((4, 128, 256), BF1...]
    all_gather x1 -> x0, blocking collectives: 40.9 us -> none  [local(): lax.all_gather(rows_view.astype(jnp.bfloat16), 'col', axis=2, tiled=True)]
    dot_general x14 -> x0, matrix products: 14.9 us -> none  [the longest x1 2.07 us: local(): jnp.einsum('axpk,kpm->xam', phases, mode_piece, precision=exact_mode)]
    unnamed x14 -> x47, local copies, waits for them, and re-layouts: 7.52 us -> 22.3 us
  transfers between devices with their start and end apart: 3 -> 0, of which waited for: 2 -> 0; matrix products, arithmetic and copies ran while one was open for 1% -> 0% of each run, Pallas kernels for 0% -> 0%
where the time goes in v1:
time: 108 us; the launch traced here: 107 us
  Pallas kernels  84.3 us (78%)
  local copies, waits for them, and re-layouts  22.3 us (21%)
    pallas_call x1, Pallas kernels, local(): pl.pallas_call(kernel, out_shape=(jax.ShapeDtypeStruct((4, 128, 256), BF1...  84.3 us
    unnamed x47, local copies, waits for them, and re-layouts  22.3 us

profile of v1, /device:TPU:1, one launch (start us, length us, event | category | flops | bytes accessed | tf_op | source)
XLA Modules:
  0.0 107.3 jit_solution(13395756158766372255)
XLA Ops:
  0.6 0.0 copy-start
  0.6 1.2 %copy-done = bf16[4,512,256]{2,1,0:T(8,128)(2,1)S(1)} copy-done((bf16[4,512,256]{2,1,0:T(8,128)(2,1)S(1)}, bf16[4,512,256]{2,1,0:T(8,128)(2,1)}, u32[]{:S(2)}) %copy-start) | copy-done | bytes 1048600
  1.9 0.0 copy-start.1
  1.9 1.1 %copy-done.1 = bf16[2,512,384]{2,1,0:T(8,128)(2,1)S(1)} copy-done((bf16[2,512,384]{2,1,0:T(8,128)(2,1)S(1)}, bf16[2,512,384]{2,1,0:T(8,128)(2,1)}, u32[]{:S(2)}) %copy-start.1) | copy-done | bytes 786456
  3.0 0.0 copy-start.2
  3.0 1.0 copy-done.2
  4.0 0.0 copy-start.3
  4.0 1.0 copy-done.3
  5.0 0.0 copy-start.4
  5.0 0.9 copy-done.4
  5.9 0.0 copy-start.5
  5.9 0.9 copy-done.5
  6.9 0.0 copy-start.6
  6.9 0.9 copy-done.6
  7.8 0.0 copy-start.7
  7.8 0.9 copy-done.7
  8.8 0.0 copy-start.8
  8.8 0.9 copy-done.8
  9.7 0.0 copy-start.9
  9.7 0.9 copy-done.9
  10.7 0.0 copy-start.10
  10.7 0.9 copy-done.10
  11.6 0.0 copy-start.11
  11.6 0.9 copy-done.11
  12.6 0.0 copy-start.12
  12.6 0.9 copy-done.12
  13.5 0.0 copy-start.13
  13.5 0.9 copy-done.13
  14.4 0.0 copy-start.14
  14.4 0.9 copy-done.14
  15.2 0.0 copy-start.15
  15.2 0.9 copy-done.15
  16.1 0.0 copy-start.16
  16.1 0.9 copy-done.16
  17.0 0.0 copy-start.17
  17.0 0.8 copy-done.17
  17.9 0.0 copy-start.18
  17.9 0.8 copy-done.18
  18.7 0.0 copy-start.19
  18.7 0.8 copy-done.19
  19.4 0.0 copy-start.20
  19.4 0.7 copy-done.20
  20.2 0.0 copy-start.21
  20.2 0.7 copy-done.21
  20.8 84.3 %fno_backward.1 = (bf16[4,128,256]{2,1,0:T(8,128)(2,1)S(1)}, f32[2,80,1024]{2,1,0:T(8,128)S(1)}, f32[32,32]{1,0:T(8,128)S(1)}) custom-call(bf16[4,128,256]{2,1,0:T(8,128)(2,1)S(1)} %copy-done.4, bf16[4,128,256]{2,1,0:T(8,128)(2,1)S(1)} %copy-done.5, bf16[4,128,256]{2,1,0:T(8,128)(2,1)S(1)} %copy-done.6, bf16[2,80,1024]{2,1,0:T(8,128)(2,1)S(1)} %bitcast.7, ...), custom_call_target="tpu_custom_call" | custom-call | tf_op jit(solution)/shard_map/fno_backward/pallas_call | solution.py:528
  105.2 0.7 copy.29
  105.9 0.8 copy.30
  106.7 0.6 copy.31
Async XLA Ops:
  0.6 1.2 %copy-start = (bf16[4,512,256]{2,1,0:T(8,128)(2,1)S(1)}, bf16[4,512,256]{2,1,0:T(8,128)(2,1)}, u32[]{:S(2)}) copy-start(bf16[4,512,256]{2,1,0:T(8,128)(2,1)} %constant.44.clone.refs_6_) | copy-start | bytes 3145732
  1.9 1.1 %copy-start.1 = (bf16[2,512,384]{2,1,0:T(8,128)(2,1)S(1)}, bf16[2,512,384]{2,1,0:T(8,128)(2,1)}, u32[]{:S(2)}) copy-start(bf16[2,512,384]{2,1,0:T(8,128)(2,1)} %constant.38.clone.refs_1_) | copy-start | bytes 2359300
  3.0 1.0 copy-start.2
  4.0 1.0 copy-start.3
  5.0 0.9 copy-start.4
  5.9 0.9 copy-start.5
  6.9 0.9 copy-start.6
  7.8 0.9 copy-start.7
  8.8 0.9 copy-start.8
  9.7 0.9 copy-start.9
  10.7 0.9 copy-start.10
  11.6 0.9 copy-start.11
  12.6 0.9 copy-start.12
  13.5 0.9 copy-start.13
  14.4 0.9 copy-start.14
  15.2 0.9 copy-start.15
  16.1 0.9 copy-start.16
  17.0 0.8 copy-start.17
  17.9 0.8 copy-start.18
  18.7 0.8 copy-start.19
  19.4 0.7 copy-start.20
  20.2 0.7 copy-start.21

commit v2 on v1

--- a/solution.py
+++ b/solution.py
@@ -46,11 +46,8 @@
         for t in range(NT):
             high[f, 0, t, :, f, 0, :] = eye * cos[t, 4]
             high[f, 1, t, :, f, 1, :] = eye * cos[t, 4]
-    forward = np.stack(
-        [
-            np.concatenate([low.reshape(512, 256), high[f].reshape(512, 128)], 1)
-            for f in range(2)
-        ]
+    forward = np.concatenate(
+        [low.reshape(512, 256), high[0].reshape(512, 128), high[1].reshape(512, 128)], 1
     )
     inverse = np.zeros((3, 4, C, 2, NT, C))
     for t in range(NT):
@@ -147,7 +144,7 @@
     group = np.arange(128) % C
     lane = np.arange(C * C)
     by_in = (group[:, None] == lane[None, :] // C).astype(np.float64)
-    by_out = (group[:, None] == lane[None, :] % C).astype(np.float64)
+    by_out = (group[:, None] == lane[None, :256] % C).astype(np.float64)
     return (
         pick.reshape(320, 128),
         pick_mask.reshape(320, 128),
@@ -168,13 +165,12 @@
     t["pick"], t["pick_m"], t["by_in"], t["by_out"], t["by_in_t"], t["spread"], t["spread_m"] = (
         mixing_tables()
     )
-    t["rep"] = (np.arange(256)[:, None] % C == np.arange(128)[None, :] % C).astype(np.float64)
     return {k: np.asarray(v, np.float32).astype(jnp.bfloat16) for k, v in t.items()}
 
 
 PICKED = ("col_f", "col_i", "row_f", "row_i")
 ORDER = (
-    "col_f", "time_f", "rep", "reg_a", "reg_b", "reg_l", "row_f", "pick", "pick_m", "by_in",
+    "col_f", "time_f", "reg_a", "reg_b", "reg_l", "row_f", "pick", "pick_m", "by_in",
     "by_out", "by_in_t", "spread", "spread_m", "row_i", "reg_c", "time_i", "col_i",
 )
 
@@ -197,22 +193,21 @@
     return (cot.astype(F32) * gelu_slope(pre.astype(F32))).astype(BF16)
 
 
-def column_time(field, col_f, time_f):
-    y = mm(col_f, field).astype(BF16)
-    return mm(jnp.concatenate([y[:64], y[64:]], axis=1), time_f)
-
-
 def group_mask(shape):
     row = lax.broadcasted_iota(jnp.int32, shape, 0)
     lane = lax.broadcasted_iota(jnp.int32, shape, 1)
     return row, lane
 
 
-def pack_bypass(product, rep):
+def fold_lanes(values):
+    values = values + pltpu.roll(values, 64, 1)
+    return values + pltpu.roll(values, 32, 1)
+
+
+def pack_bypass(product):
     row, lane = group_mask((256, 256))
-    kept = jnp.where(row // C == lane // C, product, 0.0)
-    wide = mm_full(kept, rep.astype(F32))
-    wide = wide.reshape(8, C, 128).sum(0)
+    kept = jnp.where(row // C == lane // C, product, 0.0).reshape(8, C, 256).sum(0)
+    wide = fold_lanes(kept[:, :128] + kept[:, 128:])
     row, lane = group_mask((C, 128))
     kept = jnp.where(row % 4 == lane // C, wide, 0.0)
     row, lane = group_mask((8, C))
@@ -223,9 +218,8 @@
     row, lane = group_mask((C, 8))
     wide = mm_full(jnp.where(row // 4 == lane, 1.0, 0.0), packed)
     row, lane = group_mask((C, 128))
-    kept = jnp.where(row % 4 == lane // C, wide, 0.0)
-    row, lane = group_mask((128, C))
-    return mm_full(kept, jnp.where(row % C == lane, 1.0, 0.0)) * BYPASS_SCALE
+    kept = fold_lanes(jnp.where(row % 4 == lane // C, wide, 0.0))
+    return kept[:, :C] * BYPASS_SCALE
 
 
 def block_bypass(bypass):
@@ -245,21 +239,6 @@
     return mm(reg_a, rows) + mm(reg_b, turned)
 
 
-def mixing(modes, w_re, w_im, pick, pick_m, by_in, by_out, by_in_t, spread, spread_m):
-    chosen = (mm(pick, modes) * pick_m.astype(F32)).astype(BF16)
-    a = mm(chosen[:160], by_in)
-    g = mm(chosen[160:], by_out)
-    a_re, a_im, g_re, g_im = a[:80], a[80:], g[:80], g[80:]
-    out_re = FACTOR * (a_re * g_re + a_im * g_im)
-    out_im = FACTOR * (a_re * g_im - a_im * g_re)
-    p_re = w_re * g_re + w_im * g_im
-    p_im = w_re * g_im - w_im * g_re
-    b_re = mm(p_re.astype(BF16), by_in_t) * FACTOR
-    b_im = mm(p_im.astype(BF16), by_in_t) * FACTOR
-    stack = jnp.concatenate([b_re, b_im, b_im, b_re], axis=0) * spread_m.astype(F32)
-    return out_re, out_im, mm(spread, stack.astype(BF16))
-
-
 def final_rows(low_re, low_im, high, time_i, col_i):
     z = jnp.concatenate([low_re, low_im, high], axis=1)
     u = mm(z, time_i).astype(BF16)
@@ -270,15 +249,17 @@
     return block.astype(F32).reshape(count, 128).astype(BF16)
 
 
-def kernel(inp, pre, cot, spec, byp, *refs):
+def kernel(inp_hbm, pre_hbm, cot_hbm, spec_hbm, byp_hbm, *refs):
     n = len(ORDER)
     tables = dict(zip(ORDER, refs[:n]))
-    out_g, out_s, out_b = refs[n : n + 3]
+    out_g_hbm, out_s_hbm, out_b = refs[n : n + 3]
     held = dict(zip(ORDER, refs[n + 3 : 2 * n + 3]))
     (
+        inp, pre, cot, spec, byp, out_g, out_s, arg_sem, out_sem,
         grad, plus, pieces, recv_col, send_s, recv_s, rows_all, send_x, recv_x, send_q, recv_q,
         send_b, recv_b, recv_g, send_l, recv_l, send_c, recv_c,
         sum_a, sum_b, sum_c, sum_d, by_a, by_b, by_c, by_d,
+        lined, high, product, blocks, chosen, repeated,
         table_sem, send_sem, recv_sem,
     ) = refs[2 * n + 3 :]
 
@@ -324,167 +305,276 @@
 
     index_of = {"col_f": j, "col_i": j, "row_f": xx, "row_i": xx * 2 + zh}
     loads = {}
-    for at, name in enumerate(ORDER):
+
+    def load(name):
         source = tables[name].at[index_of[name]] if name in PICKED else tables[name]
-        loads[name] = pltpu.make_async_copy(source, held[name], table_sem.at[at])
+        loads[name] = pltpu.make_async_copy(source, held[name], table_sem.at[ORDER.index(name)])
         loads[name].start()
+
+    args = []
+    for at, (source, target) in enumerate(
+        ((inp_hbm, inp), (cot_hbm, cot), (pre_hbm, pre), (byp_hbm, byp), (spec_hbm, spec))
+    ):
+        args.append(pltpu.make_async_copy(source, target, arg_sem.at[at]))
+    args[0].start()
+    load("col_f")
+    load("time_f")
+    args[1].start()
+    args[2].start()
+    args[3].start()
+    args[4].start()
+    for name in ORDER[2:]:
+        load(name)
 
     def table(name):
         return held[name][...]
 
-    sent = []
-
-    def send(source, target, peer):
-        at = len(sent)
-        copy = pltpu.make_async_remote_copy(
-            src_ref=source,
-            dst_ref=target,
-            send_sem=send_sem.at[at],
-            recv_sem=recv_sem.at[at],
-            device_id=peer,
-            device_id_type=MESH,
-        )
-        copy.start()
-        sent.append(copy)
-        return copy
-
-    def arrive(copies):
-        for copy in copies:
-            copy.wait_recv()
+    exchanges = []
+    used = [0]
+
+    def exchange(count, make):
+        base = used[0]
+        used[0] += count
+
+        def copy(k):
+            source, target, peer = make(k)
+            return pltpu.make_async_remote_copy(
+                src_ref=source,
+                dst_ref=target,
+                send_sem=send_sem.at[base + k],
+                recv_sem=recv_sem.at[base + k],
+                device_id=peer,
+                device_id_type=MESH,
+            )
+
+        def start(k, carry):
+            copy(k).start()
+            return carry
+
+        lax.fori_loop(0, count, start, 0)
+        pair = copy, count
+        exchanges.append(pair)
+        return pair
+
+    def arrive(pair, first=0, last=None):
+        copy, count = pair
+
+        def wait(k, carry):
+            copy(k).wait_recv()
+            return carry
+
+        lax.fori_loop(first, count if last is None else last, wait, 0)
 
     loads["col_f"].wait()
+    args[0].wait()
+
+    def lines_in(x, carry):
+        y = mm(held["col_f"][...], inp[x]).astype(BF16)
+        lined[x, :, 0:256] = y[:64]
+        lined[x, :, 256:512] = y[64:]
+        return carry
+
+    lax.fori_loop(0, 4, lines_in, 0)
     loads["time_f"].wait()
-    col_f = table("col_f")
-    high = []
+    r = mm(lined[...].reshape(256, 512), held["time_f"][:, 0:384])
     for x in range(4):
-        r = column_time(inp[x], col_f, held["time_f"][0])
-        pieces[:, 0, x] = r[:, :128].reshape(8, 8, 128).astype(BF16)
-        pieces[:, 1, x] = r[:, 128:256].reshape(8, 8, 128).astype(BF16)
-        high.append(r[:, 256:])
+        rows = slice(64 * x, 64 * x + 64)
+        pieces[:, 0, x] = r[rows, :128].reshape(8, 8, 128).astype(BF16)
+        pieces[:, 1, x] = r[rows, 128:256].reshape(8, 8, 128).astype(BF16)
+    high[...] = r[:, 256:]
     pl.semaphore_wait(barrier, len(everyone))
-    first = []
-    for k in range(1, 8):
-        to = (j + k) % 8
-        first.append(send(pieces.at[to, 0:2], recv_col.at[k - 1, 0:2], col_peer(k)))
-    for x in range(4):
+    first_in = exchange(
+        7,
+        lambda k: (
+            pieces.at[(j + k + 1) % 8, 0:2],
+            recv_col.at[k, 0:2],
+            col_peer(k + 1),
+        ),
+    )
+    args[1].wait()
+    args[2].wait()
+
+    def lines_grad(x, carry):
         g = pre_gradient(cot[x], pre[x])
         grad[x] = g
-        r = column_time(g, col_f, held["time_f"][1])
-        pieces[:, 2, x] = r[:, :128].reshape(8, 8, 128).astype(BF16)
-        pieces[:, 3, x] = r[:, 128:256].reshape(8, 8, 128).astype(BF16)
-        pieces[:, 4, x] = (high[x] + r[:, 256:]).reshape(8, 8, 128).astype(BF16)
-    for k in range(1, 8):
-        to = (j + k) % 8
-        first.append(send(pieces.at[to, 2:5], recv_col.at[k - 1, 2:5], col_peer(k)))
-
-    product = jnp.zeros((256, 256), F32)
+        y = mm(held["col_f"][...], g).astype(BF16)
+        lined[x, :, 0:256] = y[:64]
+        lined[x, :, 256:512] = y[64:]
+        return carry
+
+    lax.fori_loop(0, 4, lines_grad, 0)
+    rows = lined[...].reshape(256, 512)
+    r = mm(rows, held["time_f"][:, 0:256])
+    top = high[...] + mm(rows, held["time_f"][:, 384:512])
     for x in range(4):
-        product += lax.dot_general(
+        rows = slice(64 * x, 64 * x + 64)
+        pieces[:, 2, x] = r[rows, :128].reshape(8, 8, 128).astype(BF16)
+        pieces[:, 3, x] = r[rows, 128:].reshape(8, 8, 128).astype(BF16)
+        pieces[:, 4, x] = top[rows].reshape(8, 8, 128).astype(BF16)
+    first_grad = exchange(
+        7,
+        lambda k: (
+            pieces.at[(j + k + 1) % 8, 2:5],
+            recv_col.at[k, 2:5],
+            col_peer(k + 1),
+        ),
+    )
+
+    product[...] = jnp.zeros((256, 256), F32)
+
+    def add_product(x, carry):
+        product[...] += lax.dot_general(
             inp[x], grad[x], (((0,), (0,)), ((), ())), preferred_element_type=F32
         )
-    loads["rep"].wait()
-    by_a[j] = pack_bypass(product, table("rep"))
-    bypass_a = [send(by_a.at[j], by_a.at[j], col_peer(k)) for k in range(1, 8)]
-    blocks = block_bypass(byp[...])
-    for x in range(4):
-        plus[x] = mm(grad[x], blocks)
+        return carry
+
+    lax.fori_loop(0, 4, add_product, 0)
+    by_a[j] = pack_bypass(product[...])
+    bypass_a = exchange(7, lambda k: (by_a.at[j], by_a.at[j], col_peer(k + 1)))
+    args[3].wait()
+    blocks[...] = block_bypass(byp[...])
+
+    def pointwise(x, carry):
+        plus[x] = mm(grad[x], blocks[...])
+        return carry
+
+    lax.fori_loop(0, 4, pointwise, 0)
 
     for name in ("reg_a", "reg_b", "reg_l"):
         loads[name].wait()
-    arrive(first)
+    arrive(first_in)
+    arrive(first_grad)
     total = pieces[j].astype(F32).reshape(160, 128)
     for k in range(7):
         total += recv_col[k].astype(F32).reshape(160, 128)
     grouped = regroup_forward(total, table("reg_a"), table("reg_b"), table("reg_l"))
     send_s[...] = grouped.reshape(8, 3, 8, 128).astype(BF16)
     recv_s[s] = send_s[s]
-    second = [send(send_s.at[s_index(k)], recv_s.at[s], s_peer(k)) for k in range(1, 8)]
+    second = exchange(7, lambda k: (send_s.at[s_index(k + 1)], recv_s.at[s], s_peer(k + 1)))
 
     arrive(bypass_a)
     by_b[s] = by_a[...].sum(0)
-    bypass_b = [send(by_b.at[s], by_b.at[s], s_peer(k)) for k in range(1, 8)]
+    bypass_b = exchange(7, lambda k: (by_b.at[s], by_b.at[s], s_peer(k + 1)))
 
     arrive(second)
+    third_a = exchange(1, lambda k: (recv_s.at[:, 1 - zh], rows_all.at[0, zh], zh_peer()))
+    third_b = exchange(1, lambda k: (recv_s.at[:, 2], rows_all.at[1, zh], zh_peer()))
     rows_all[0, zh] = recv_s[:, zh]
     rows_all[1, zh] = recv_s[:, 2]
-    third = [
-        send(recv_s.at[:, 1 - zh], rows_all.at[0, zh], zh_peer()),
-        send(recv_s.at[:, 2], rows_all.at[1, zh], zh_peer()),
-    ]
     arrive(bypass_b)
     by_c[zh] = by_b[...].sum(0)
-    bypass_c = [send(by_c.at[zh], by_c.at[zh], zh_peer())]
+    bypass_c = exchange(1, lambda k: (by_c.at[zh], by_c.at[zh], zh_peer()))
 
     loads["row_f"].wait()
-    arrive(third)
+    arrive(third_a)
+    arrive(third_b)
     partial = mm(table("row_f"), rows_of(rows_all[...], 256))
     send_x[...] = partial.reshape(4, 16, 8, 128).astype(BF16)
-    fourth = [
-        send(send_x.at[(xx + k) % 4], recv_x.at[k - 1], x_peer(k)) for k in range(1, 4)
-    ]
+    fourth = exchange(
+        3, lambda k: (send_x.at[(xx + k + 1) % 4], recv_x.at[k], x_peer(k + 1))
+    )
     arrive(bypass_c)
     by_d[xx] = by_c[...].sum(0)
-    bypass_d = [send(by_d.at[xx], by_d.at[xx], x_peer(k)) for k in range(1, 4)]
+    bypass_d = exchange(3, lambda k: (by_d.at[xx], by_d.at[xx], x_peer(k + 1)))
     arrive(fourth)
     summed = send_x[xx].astype(F32)
     for k in range(3):
         summed += recv_x[k].astype(F32)
     send_q[...] = summed.astype(BF16)
 
+    fifth = exchange(15, lambda k: (send_q.at[q_index(k + 1)], recv_q.at[q], q_peer(k + 1)))
     recv_q[q] = send_q[q]
-    fifth = [send(send_q.at[q_index(k)], recv_q.at[q], q_peer(k)) for k in range(1, 16)]
     for name in ("pick", "pick_m", "by_in", "by_out", "by_in_t", "spread", "spread_m"):
         loads[name].wait()
+    args[4].wait()
     arrive(bypass_d)
     out_b[...] = unpack_bypass(by_d[...].sum(0))
     arrive(fifth)
-    out_re, out_im, back = mixing(
-        rows_of(recv_q[...], 128),
-        spec[0].astype(F32),
-        spec[1].astype(F32),
-        *[
-            table(name)
-            for name in ("pick", "pick_m", "by_in", "by_out", "by_in_t", "spread", "spread_m")
-        ],
-    )
+    chosen[...] = (mm(table("pick"), rows_of(recv_q[...], 128)) * table("pick_m").astype(F32)).astype(BF16)
+    repeated[...] = mm(chosen[160:320, :], table("by_out"))
+
+    def mix(m, carry):
+        lanes = pl.ds(pl.multiple_of(m * 256, 256), 256)
+        a = mm(chosen[0:160, :], held["by_in"][:, lanes])
+        a_re, a_im = a[:80], a[80:]
+        g_re = repeated[0:80, :]
+        g_im = repeated[80:160, :]
+        w_re = spec[0, :, lanes].astype(F32)
+        w_im = spec[1, :, lanes].astype(F32)
+        out_s[0, :, lanes] = FACTOR * (a_re * g_re + a_im * g_im)
+        out_s[1, :, lanes] = FACTOR * (a_re * g_im - a_im * g_re)
+        p_re = (w_re * g_re + w_im * g_im).astype(BF16)
+        p_im = (w_re * g_im - w_im * g_re).astype(BF16)
+        turn = held["by_in_t"][lanes, :]
+        return carry + mm(jnp.concatenate([p_re, p_im], axis=0), turn)
+
+    b = lax.fori_loop(0, 4, mix, jnp.zeros((160, 128), F32)) * FACTOR
+    b_re, b_im = b[:80], b[80:]
+    stack = jnp.concatenate([b_re, b_im, b_im, b_re], axis=0) * table("spread_m").astype(F32)
+    back = mm(table("spread"), stack.astype(BF16))
     send_b[...] = back.reshape(8, 8, 128).astype(BF16)
+
+    def mode_home(k):
+        to = q_index(k + 1)
+        return send_b.at[(to // 4) * 2 + to % 2], recv_b.at[q], q_peer(k + 1)
+
+    sixth = exchange(15, mode_home)
     recv_b[q] = send_b[s]
-    sixth = []
-    for k in range(1, 16):
-        to = q_index(k)
-        sixth.append(send(send_b.at[(to // 4) * 2 + to % 2], recv_b.at[q], q_peer(k)))
-    out_s[0] = out_re
-    out_s[1] = out_im
+    out_copy_s = pltpu.make_async_copy(out_s, out_s_hbm, out_sem.at[4])
+    out_copy_s.start()
 
     arrive(sixth)
+    seventh = exchange(3, lambda k: (recv_b, recv_g.at[xx], x_peer(k + 1)))
     recv_g[xx] = recv_b[...]
-    seventh = [send(recv_b, recv_g.at[xx], x_peer(k)) for k in range(1, 4)]
     loads["row_i"].wait()
     loads["reg_c"].wait()
     arrive(seventh)
     lines = mm(table("row_i"), rows_of(recv_g[...], 512))
     send_l[...] = lines.reshape(8, 16, 128).astype(BF16)
+    eighth = exchange(7, lambda k: (send_l.at[s_index(k + 1)], recv_l.at[s], s_peer(k + 1)))
     recv_l[s] = send_l[s]
-    eighth = [send(send_l.at[s_index(k)], recv_l.at[s], s_peer(k)) for k in range(1, 8)]
     arrive(eighth)
     turned = mm(table("reg_c"), rows_of(recv_l[...], 128))
     send_c[...] = turned.reshape(4, 3, 8, 128).astype(BF16)
+    ninth = exchange(
+        14,
+        lambda k: (
+            send_c.at[pl.ds((k // 7) * 2, 2)],
+            recv_c.at[j, pl.ds((k // 7) * 2, 2)],
+            col_peer(k % 7 + 1),
+        ),
+    )
     recv_c[j] = send_c[...]
-    ninth = [send(send_c, recv_c.at[j], col_peer(k)) for k in range(1, 8)]
     loads["time_i"].wait()
     loads["col_i"].wait()
-    time_i = table("time_i")
-    col_i = table("col_i")
-    arrive(ninth)
+
+    def out_copy(x):
+        return pltpu.make_async_copy(out_g.at[x], out_g_hbm.at[x], out_sem.at[x])
+
+    def final(x, carry):
+        parts = [rows_of(recv_c[:, x, tile], 64) for tile in range(3)]
+        rows = final_rows(*parts, held["time_i"][...], held["col_i"][...])
+        out_g[x] = (rows + plus[x]).astype(BF16)
+        out_copy(x).start()
+        return carry
+
+    for half in range(2):
+        arrive(ninth, 7 * half, 7 * half + 7)
+        lax.fori_loop(2 * half, 2 * half + 2, final, 0)
+
+    for copy, count in exchanges:
+
+        def drain(k, carry, copy=copy):
+            copy(k).wait_send()
+            return carry
+
+        lax.fori_loop(0, count, drain, 0)
     for x in range(4):
-        parts = [rows_of(recv_c[:, x, tile], 64) for tile in range(3)]
-        out_g[x] = (final_rows(*parts, time_i, col_i) + plus[x]).astype(BF16)
-
-    for copy in sent:
-        copy.wait_send()
-
-
-N_COPIES = 14 + 7 + 7 + 7 + 2 + 1 + 3 + 3 + 15 + 15 + 3 + 7 + 7
+        out_copy(x).wait()
+    out_copy_s.wait()
+
+
+N_COPIES = 14 + 7 + 7 + 7 + 2 + 1 + 3 + 3 + 15 + 15 + 3 + 7 + 14
 
 
 def local(inputs, preactivation, cotangent, spectral, bypass, tables):
@@ -495,6 +585,15 @@
         pltpu.VMEM(tables[k].shape[1:] if k in PICKED else tables[k].shape, BF16) for k in ORDER
     ]
     blocks = [
+        pltpu.VMEM((4, 128, 256), BF16),
+        pltpu.VMEM((4, 128, 256), BF16),
+        pltpu.VMEM((4, 128, 256), BF16),
+        pltpu.VMEM((2, 80, C * C), BF16),
+        pltpu.VMEM((C, C), BF16),
+        pltpu.VMEM((4, 128, 256), BF16),
+        pltpu.VMEM((2, 80, C * C), F32),
+        pltpu.SemaphoreType.DMA((5,)),
+        pltpu.SemaphoreType.DMA((5,)),
         pltpu.VMEM((4, 128, 256), BF16),
         pltpu.VMEM((4, 128, 256), F32),
         pltpu.VMEM((8, 5, 4, 8, 128), BF16),
@@ -521,6 +620,12 @@
         pltpu.VMEM((8, 8, 128), F32),
         pltpu.VMEM((2, 8, 128), F32),
         pltpu.VMEM((4, 8, 128), F32),
+        pltpu.VMEM((4, 64, 512), BF16),
+        pltpu.VMEM((256, 128), F32),
+        pltpu.VMEM((256, 256), F32),
+        pltpu.VMEM((256, 256), BF16),
+        pltpu.VMEM((320, 128), BF16),
+        pltpu.VMEM((160, 256), F32),
         pltpu.SemaphoreType.DMA((len(ORDER),)),
         pltpu.SemaphoreType.DMA((N_COPIES,)),
         pltpu.SemaphoreType.DMA((N_COPIES,)),
@@ -532,11 +637,11 @@
             jax.ShapeDtypeStruct((2, 80, C * C), F32),
             jax.ShapeDtypeStruct((C, C), F32),
         ),
-        in_specs=[vmem] * 5 + [anywhere] * len(ORDER),
-        out_specs=(vmem, vmem, vmem),
+        in_specs=[anywhere] * (5 + len(ORDER)),
+        out_specs=(anywhere, anywhere, vmem),
         scratch_shapes=held + blocks,
         compiler_params=pltpu.CompilerParams(
-            collective_id=0, has_side_effects=True, vmem_limit_bytes=48 * 1024 * 1024
+            collective_id=0, has_side_effects=True, vmem_limit_bytes=62 * 1024 * 1024
         ),
         name="fno_backward",
     )(inputs, preactivation, cotangent, weight, bypass, *[tables[k] for k in ORDER])

time: 108 us -> 93.2 us (0.86)
  local copies, waits for them, and re-layouts: 22.3 us -> 4.28 us
  Pallas kernels: 84.3 us -> 88.1 us
    unnamed x47 -> x5, local copies, waits for them, and re-layouts: 22.3 us -> 4.28 us
    pallas_call x1, Pallas kernels: 84.3 us -> 88.1 us  [local(): pl.pallas_call(kernel, out_shape=(jax.ShapeDtypeStruct((4, 128, 256), BF1...]
where the time goes in v2:
time: 93.2 us; the launch traced here: 93 us
  Pallas kernels  88.1 us (95%)
  local copies, waits for them, and re-layouts  4.28 us (5%)
    pallas_call x1, Pallas kernels, local(): pl.pallas_call(kernel, out_shape=(jax.ShapeDtypeStruct((4, 128, 256), BF1...  88.1 us
    unnamed x5, local copies, waits for them, and re-layouts  4.28 us

profile of v2, /device:TPU:1, one launch (start us, length us, event | category | flops | bytes accessed | tf_op | source)
XLA Modules:
  0.0 93.0 jit_solution(10273438892844092359)
XLA Ops:
  0.6 88.1 %fno_backward.1 = (bf16[4,128,256]{2,1,0:T(8,128)(2,1)}, f32[2,80,1024]{2,1,0:T(8,128)}, f32[32,32]{1,0:T(8,128)}) custom-call(bf16[4,128,256]{2,1,0:T(8,128)(2,1)} %inp_hbm.1, bf16[4,128,256]{2,1,0:T(8,128)(2,1)} %pre_hbm.1, bf16[4,128,256]{2,1,0:T(8,128)(2,1)} %cot_hbm.1, bf16[2,80,1024]{2,1,0:T(8,128)(2,1)} %bitcast.7, bf16[32,32]{1,0:T(8,128)(2,1)} %byp_hbm.1, ...), custom_call_target="tpu_custom_call" | custom-call | tf_op jit(solution)/shard_map/fno_backward/pallas_call | solution.py:633
  88.7 1.7 %copy.28 = bf16[4,128,256]{2,1,0:T(8,128)(2,1)} copy(bf16[4,128,256]{2,1,0:T(8,128)(2,1)} %get-tuple-element.12) | data formatting | bytes 524288
  90.4 0.0 copy-start
  90.4 2.0 %copy.29 = f32[2,2,8,5,1024]{4,2,3,1,0:T(8,128)} copy(f32[2,2,8,5,1024]{4,2,3,1,0:T(8,128)} %bitcast.6) | data formatting | bytes 1310720
  92.4 0.0 copy-done
  92.4 0.6 copy.30
Async XLA Ops:
  90.4 2.0 %copy-start = (f32[32,32]{1,0:T(8,128)S(1)}, f32[32,32]{1,0:T(8,128)}, u32[]{:S(2)}) copy-start(f32[32,32]{1,0:T(8,128)} %get-tuple-element.14) | copy-start | bytes 12292

commit v3 on v2

--- a/solution.py
+++ b/solution.py
@@ -90,16 +90,23 @@
     cos, sin = turns(freq, np.arange(NX), NX)
     cos = cos.reshape(4, 16, 2, 4, 4, 2, 2, 4)
     sin = sin.reshape(4, 16, 2, 4, 4, 2, 2, 4)
-    forward = np.zeros((4, 4, 16, 2, 2, 2, 2, 2, 4, 2, 2, 4))
+    forward = np.zeros((4, 2, 4, 16, 2, 2, 4, 2, 2, 4))
     for xx in range(4):
-        for slab in range(2):
-            c = cos[:, :, :, xx].transpose(0, 1, 2, 4, 3, 5, 6)
-            s = sin[:, :, :, xx].transpose(0, 1, 2, 4, 3, 5, 6)
-            forward[xx, :, :, slab, :, 0, slab, :, :, :, 0, :] = c
-            forward[xx, :, :, slab, :, 0, slab, :, :, :, 1, :] = s
-            forward[xx, :, :, slab, :, 1, slab, :, :, :, 1, :] = c
-            forward[xx, :, :, slab, :, 1, slab, :, :, :, 0, :] = -s
-    forward = forward.reshape(4, 512, 256)
+        for zh in range(2):
+            c = cos[:, :, :, xx, :, zh]
+            s = sin[:, :, :, xx, :, zh]
+            forward[xx, zh, :, :, :, 0, :, :, 0, :] = c
+            forward[xx, zh, :, :, :, 0, :, :, 1, :] = s
+            forward[xx, zh, :, :, :, 1, :, :, 1, :] = c
+            forward[xx, zh, :, :, :, 1, :, :, 0, :] = -s
+    forward = forward.reshape(8, 256, 64)
+    deal = np.zeros((16, 16, 3, 16, 2, 2))
+    for q in range(16):
+        for e in range(2):
+            for ab in range(2):
+                for slab in range(2):
+                    deal[q, slab * 4 + e * 2 + ab, slab, q, e, ab] = 1.0
+            deal[q, 8 + e, 2, q, e, 0] = 1.0
     inverse = np.zeros((4, 2, 4, 2, 2, 2, 4, 4, 16, 2, 2, 2))
     for xx in range(4):
         for zh in range(2):
@@ -110,24 +117,25 @@
                 inverse[xx, zh, :, :, slab, 0, :, :, :, slab, :, 1] = -s
                 inverse[xx, zh, :, :, slab, 1, :, :, :, slab, :, 1] = c
                 inverse[xx, zh, :, :, slab, 1, :, :, :, slab, :, 0] = s
-    return forward, inverse.reshape(8, 128, 512)
+    return forward, inverse.reshape(8, 128, 512), deal.reshape(256, 192)
 
 
 def mixing_tables():
-    pick = np.zeros((2, 2, 2, 5, 8, 16, 2, 2, 2))
+    pick = np.zeros((2, 2, 2, 5, 8, 16, 16))
     pick_mask = np.zeros((2, 2, 2, 5, 8, 4, C))
     spread = np.zeros((8, 2, 2, 2, 4, 2, 5, 8))
     spread_mask = np.zeros((4, 2, 5, 8, 4, C))
     for ky in range(8):
         for e in range(2):
             for f in range(2):
-                source = (ky // 2) * 4 + f * 2 + ky % 2
                 for ri in range(2):
                     for kt in range(4):
-                        pick[f, ri, e, kt, ky, source, 0, e, ri] = 1.0
                         pick_mask[f, ri, e, kt, ky, kt, :] = 1.0
-                    pick[f, ri, e, 4, ky, source, 1, e, 0] = 1.0
                     pick_mask[f, ri, e, 4, ky, f * 2 + ri, :] = 1.0
+                    for zh in range(2):
+                        source = (ky // 2) * 4 + zh * 2 + ky % 2
+                        pick[f, ri, e, 0:4, ky, source, f * 4 + e * 2 + ri] = 1.0
+                        pick[f, ri, e, 4, ky, source, 8 + e] = 1.0
             for kt in range(4):
                 spread_mask[0, e, kt, ky, kt] = 1.0
                 spread_mask[1, e, kt, ky, kt] = 1.0
@@ -146,7 +154,7 @@
     by_in = (group[:, None] == lane[None, :] // C).astype(np.float64)
     by_out = (group[:, None] == lane[None, :256] % C).astype(np.float64)
     return (
-        pick.reshape(320, 128),
+        pick.reshape(320, 256),
         pick_mask.reshape(320, 128),
         by_in,
         by_out,
@@ -161,7 +169,7 @@
     t["col_f"], t["col_i"] = column_tables()
     t["time_f"], t["time_i"] = time_tables()
     t["reg_a"], t["reg_b"], t["reg_l"], t["reg_c"] = regroup_tables()
-    t["row_f"], t["row_i"] = row_tables()
+    t["row_f"], t["row_i"], t["deal"] = row_tables()
     t["pick"], t["pick_m"], t["by_in"], t["by_out"], t["by_in_t"], t["spread"], t["spread_m"] = (
         mixing_tables()
     )
@@ -170,7 +178,7 @@
 
 PICKED = ("col_f", "col_i", "row_f", "row_i")
 ORDER = (
-    "col_f", "time_f", "reg_a", "reg_b", "reg_l", "row_f", "pick", "pick_m", "by_in",
+    "col_f", "time_f", "reg_a", "reg_b", "reg_l", "row_f", "deal", "pick", "pick_m", "by_in",
     "by_out", "by_in_t", "spread", "spread_m", "row_i", "reg_c", "time_i", "col_i",
 )
 
@@ -256,9 +264,9 @@
     held = dict(zip(ORDER, refs[n + 3 : 2 * n + 3]))
     (
         inp, pre, cot, spec, byp, out_g, out_s, arg_sem, out_sem,
-        grad, plus, pieces, recv_col, send_s, recv_s, rows_all, send_x, recv_x, send_q, recv_q,
+        grad, plus, pieces, recv_col, send_s, recv_s, send_x, recv_x, send_q, recv_q,
         send_b, recv_b, recv_g, send_l, recv_l, send_c, recv_c,
-        sum_a, sum_b, sum_c, sum_d, by_a, by_b, by_c, by_d,
+        by_sum, wide_q, by_a, by_b, by_c, by_d, by_e,
         lined, high, product, blocks, chosen, repeated,
         table_sem, send_sem, recv_sem,
     ) = refs[2 * n + 3 :]
@@ -303,7 +311,7 @@
     for peer in everyone:
         pl.semaphore_signal(barrier, inc=1, device_id=peer, device_id_type=MESH)
 
-    index_of = {"col_f": j, "col_i": j, "row_f": xx, "row_i": xx * 2 + zh}
+    index_of = {"col_f": j, "col_i": j, "row_f": xx * 2 + zh, "row_i": xx * 2 + zh}
     loads = {}
 
     def load(name):
@@ -429,8 +437,8 @@
         return carry
 
     lax.fori_loop(0, 4, add_product, 0)
-    by_a[j] = pack_bypass(product[...])
-    bypass_a = exchange(7, lambda k: (by_a.at[j], by_a.at[j], col_peer(k + 1)))
+    by_a[s] = pack_bypass(product[...])
+    bypass_a = exchange(7, lambda k: (by_a.at[s], by_a.at[s], s_peer(k + 1)))
     args[3].wait()
     blocks[...] = block_bypass(byp[...])
 
@@ -453,44 +461,40 @@
     second = exchange(7, lambda k: (send_s.at[s_index(k + 1)], recv_s.at[s], s_peer(k + 1)))
 
     arrive(bypass_a)
-    by_b[s] = by_a[...].sum(0)
-    bypass_b = exchange(7, lambda k: (by_b.at[s], by_b.at[s], s_peer(k + 1)))
-
+    by_sum[...] = by_a[...].sum(0)
+    by_b[xx] = by_sum[pl.ds(s, 1), :]
+    bypass_b = exchange(3, lambda k: (by_b.at[xx], by_b.at[xx], x_peer(k + 1)))
+
+    wide_q[...] = jnp.zeros((16, 16, 128), F32)
+    loads["row_f"].wait()
+    loads["deal"].wait()
     arrive(second)
-    third_a = exchange(1, lambda k: (recv_s.at[:, 1 - zh], rows_all.at[0, zh], zh_peer()))
-    third_b = exchange(1, lambda k: (recv_s.at[:, 2], rows_all.at[1, zh], zh_peer()))
-    rows_all[0, zh] = recv_s[:, zh]
-    rows_all[1, zh] = recv_s[:, 2]
-    arrive(bypass_b)
-    by_c[zh] = by_b[...].sum(0)
-    bypass_c = exchange(1, lambda k: (by_c.at[zh], by_c.at[zh], zh_peer()))
-
-    loads["row_f"].wait()
-    arrive(third_a)
-    arrive(third_b)
-    partial = mm(table("row_f"), rows_of(rows_all[...], 256))
-    send_x[...] = partial.reshape(4, 16, 8, 128).astype(BF16)
+    rows = jnp.concatenate([rows_of(recv_s[:, slab], 64) for slab in range(3)], axis=1)
+    send_x[...] = mm(table("row_f"), rows).reshape(4, 64, 384).astype(BF16)
     fourth = exchange(
         3, lambda k: (send_x.at[(xx + k + 1) % 4], recv_x.at[k], x_peer(k + 1))
     )
-    arrive(bypass_c)
-    by_d[xx] = by_c[...].sum(0)
-    bypass_d = exchange(3, lambda k: (by_d.at[xx], by_d.at[xx], x_peer(k + 1)))
+    arrive(bypass_b)
+    by_c[j] = by_b[...].sum(0)
+    bypass_c = exchange(7, lambda k: (by_c.at[j], by_c.at[j], col_peer(k + 1)))
     arrive(fourth)
     summed = send_x[xx].astype(F32)
     for k in range(3):
         summed += recv_x[k].astype(F32)
-    send_q[...] = summed.astype(BF16)
+    summed = summed.astype(BF16)
+    summed = jnp.concatenate([summed[:, 128 * i : 128 * i + 128] for i in range(3)], axis=0)
+    dealt = mm(table("deal"), summed).reshape(16, 16, 128)
+    send_q[...] = dealt[:, 0:10].astype(BF16)
 
     fifth = exchange(15, lambda k: (send_q.at[q_index(k + 1)], recv_q.at[q], q_peer(k + 1)))
     recv_q[q] = send_q[q]
     for name in ("pick", "pick_m", "by_in", "by_out", "by_in_t", "spread", "spread_m"):
         loads[name].wait()
     args[4].wait()
-    arrive(bypass_d)
-    out_b[...] = unpack_bypass(by_d[...].sum(0))
     arrive(fifth)
-    chosen[...] = (mm(table("pick"), rows_of(recv_q[...], 128)) * table("pick_m").astype(F32)).astype(BF16)
+    wide_q[:, 0:10] = recv_q[...].astype(F32)
+    halves = wide_q[...].reshape(256, 128).astype(BF16)
+    chosen[...] = (mm(table("pick"), halves) * table("pick_m").astype(F32)).astype(BF16)
     repeated[...] = mm(chosen[160:320, :], table("by_out"))
 
     def mix(m, carry):
@@ -522,6 +526,9 @@
     recv_b[q] = send_b[s]
     out_copy_s = pltpu.make_async_copy(out_s, out_s_hbm, out_sem.at[4])
     out_copy_s.start()
+    arrive(bypass_c)
+    by_d[zh] = by_c[...].sum(0)
+    bypass_d = exchange(1, lambda k: (by_d.at[zh], by_d.at[zh], zh_peer()))
 
     arrive(sixth)
     seventh = exchange(3, lambda k: (recv_b, recv_g.at[xx], x_peer(k + 1)))
@@ -533,6 +540,9 @@
     send_l[...] = lines.reshape(8, 16, 128).astype(BF16)
     eighth = exchange(7, lambda k: (send_l.at[s_index(k + 1)], recv_l.at[s], s_peer(k + 1)))
     recv_l[s] = send_l[s]
+    arrive(bypass_d)
+    by_e[s] = by_d[...].sum(0)
+    bypass_e = exchange(7, lambda k: (by_e.at[s], by_e.at[s], s_peer(k + 1)))
     arrive(eighth)
     turned = mm(table("reg_c"), rows_of(recv_l[...], 128))
     send_c[...] = turned.reshape(4, 3, 8, 128).astype(BF16)
@@ -547,6 +557,8 @@
     recv_c[j] = send_c[...]
     loads["time_i"].wait()
     loads["col_i"].wait()
+    arrive(bypass_e)
+    out_b[...] = unpack_bypass(by_e[...].reshape(8, 128))
 
     def out_copy(x):
         return pltpu.make_async_copy(out_g.at[x], out_g_hbm.at[x], out_sem.at[x])
@@ -574,7 +586,7 @@
     out_copy_s.wait()
 
 
-N_COPIES = 14 + 7 + 7 + 7 + 2 + 1 + 3 + 3 + 15 + 15 + 3 + 7 + 14
+N_COPIES = 14 + 7 + 3 + 7 + 1 + 7 + 7 + 3 + 15 + 15 + 3 + 7 + 14
 
 
 def local(inputs, preactivation, cotangent, spectral, bypass, tables):
@@ -600,11 +612,10 @@
         pltpu.VMEM((7, 5, 4, 8, 128), BF16),
         pltpu.VMEM((8, 3, 8, 128), BF16),
         pltpu.VMEM((8, 3, 8, 128), BF16),
-        pltpu.VMEM((2, 2, 8, 8, 128), BF16),
-        pltpu.VMEM((4, 16, 8, 128), BF16),
-        pltpu.VMEM((3, 16, 8, 128), BF16),
-        pltpu.VMEM((16, 8, 128), BF16),
-        pltpu.VMEM((16, 8, 128), BF16),
+        pltpu.VMEM((4, 64, 384), BF16),
+        pltpu.VMEM((3, 64, 384), BF16),
+        pltpu.VMEM((16, 10, 128), BF16),
+        pltpu.VMEM((16, 10, 128), BF16),
         pltpu.VMEM((8, 8, 128), BF16),
         pltpu.VMEM((16, 8, 128), BF16),
         pltpu.VMEM((4, 16, 8, 128), BF16),
@@ -613,13 +624,12 @@
         pltpu.VMEM((4, 3, 8, 128), BF16),
         pltpu.VMEM((8, 4, 3, 8, 128), BF16),
         pltpu.VMEM((8, 128), F32),
-        pltpu.VMEM((8, 128), F32),
-        pltpu.VMEM((8, 128), F32),
-        pltpu.VMEM((8, 128), F32),
+        pltpu.VMEM((16, 16, 128), F32),
         pltpu.VMEM((8, 8, 128), F32),
-        pltpu.VMEM((8, 8, 128), F32),
-        pltpu.VMEM((2, 8, 128), F32),
-        pltpu.VMEM((4, 8, 128), F32),
+        pltpu.VMEM((4, 1, 128), F32),
+        pltpu.VMEM((8, 1, 128), F32),
+        pltpu.VMEM((2, 1, 128), F32),
+        pltpu.VMEM((8, 1, 128), F32),
         pltpu.VMEM((4, 64, 512), BF16),
         pltpu.VMEM((256, 128), F32),
         pltpu.VMEM((256, 256), F32),

time: 93.2 us -> 89.4 us (0.959)
  Pallas kernels: 88.1 us -> 83.6 us
    pallas_call x1, Pallas kernels: 88.1 us -> 83.6 us  [local(): pl.pallas_call(kernel, out_shape=(jax.ShapeDtypeStruct((4, 128, 256), BF1...]
where the time goes in v3:
time: 89.4 us; the launch traced here: 88.5 us
  Pallas kernels  83.6 us (94%)
  local copies, waits for them, and re-layouts  4.28 us (5%)
    pallas_call x1, Pallas kernels, local(): pl.pallas_call(kernel, out_shape=(jax.ShapeDtypeStruct((4, 128, 256), BF1...  83.6 us
    unnamed x5, local copies, waits for them, and re-layouts  4.28 us

profile of v3, /device:TPU:1, one launch (start us, length us, event | category | flops | bytes accessed | tf_op | source)
XLA Modules:
  0.0 88.5 jit_solution(16481985687968897355)
XLA Ops:
  0.6 83.6 %fno_backward.1 = (bf16[4,128,256]{2,1,0:T(8,128)(2,1)}, f32[2,80,1024]{2,1,0:T(8,128)}, f32[32,32]{1,0:T(8,128)}) custom-call(bf16[4,128,256]{2,1,0:T(8,128)(2,1)} %inp_hbm.1, bf16[4,128,256]{2,1,0:T(8,128)(2,1)} %pre_hbm.1, bf16[4,128,256]{2,1,0:T(8,128)(2,1)} %cot_hbm.1, bf16[2,80,1024]{2,1,0:T(8,128)(2,1)} %bitcast.7, bf16[32,32]{1,0:T(8,128)(2,1)} %byp_hbm.1, ...), custom_call_target="tpu_custom_call" | custom-call | tf_op jit(solution)/shard_map/fno_backward/pallas_call | solution.py:643
  84.2 1.7 %copy.29 = bf16[4,128,256]{2,1,0:T(8,128)(2,1)} copy(bf16[4,128,256]{2,1,0:T(8,128)(2,1)} %get-tuple-element.12) | data formatting | bytes 524288
  85.9 0.0 copy-start
  85.9 2.0 %copy.30 = f32[2,2,8,5,1024]{4,2,3,1,0:T(8,128)} copy(f32[2,2,8,5,1024]{4,2,3,1,0:T(8,128)} %bitcast.6) | data formatting | bytes 1310720
  87.9 0.0 copy-done
  87.9 0.6 copy.31
Async XLA Ops:
  85.9 2.0 %copy-start = (f32[32,32]{1,0:T(8,128)S(1)}, f32[32,32]{1,0:T(8,128)}, u32[]{:S(2)}) copy-start(f32[32,32]{1,0:T(8,128)} %get-tuple-element.14) | copy-start | bytes 12292

commit v4 on v3

--- a/solution.py
+++ b/solution.py
@@ -286,26 +286,23 @@
     def s_index(k):
         return (s + k) % 8
 
-    def s_peer(k):
-        other = s_index(k)
-        return xx * 16 + (other // 2) * 4 + zh * 2 + other % 2, j
+    def q_of(other, half):
+        return (other // 2) * 4 + half * 2 + other % 2
+
+    def s_peer(k, half=zh):
+        return xx * 16 + q_of(s_index(k), half), j
 
     def zh_peer():
-        return xx * 16 + yy * 4 + (1 - zh) * 2 + core, j
+        return s_peer(0, 1 - zh)
 
     def x_peer(k):
         return ((xx + k) % 4) * 16 + q, j
-
-    def q_index(k):
-        return (q + k) % 16
-
-    def q_peer(k):
-        return xx * 16 + q_index(k), j
 
     barrier = pltpu.get_barrier_semaphore()
     everyone = (
         [col_peer(k) for k in range(1, 8)]
-        + [q_peer(k) for k in range(1, 16)]
+        + [s_peer(k) for k in range(1, 8)]
+        + [s_peer(k, 1 - zh) for k in range(8)]
         + [x_peer(k) for k in range(1, 4)]
     )
     for peer in everyone:
@@ -486,12 +483,18 @@
     dealt = mm(table("deal"), summed).reshape(16, 16, 128)
     send_q[...] = dealt[:, 0:10].astype(BF16)
 
-    fifth = exchange(15, lambda k: (send_q.at[q_index(k + 1)], recv_q.at[q], q_peer(k + 1)))
+    fifth_far = exchange(
+        8, lambda k: (send_q.at[q_of(s_index(k), 1 - zh)], recv_q.at[q], s_peer(k, 1 - zh))
+    )
+    fifth = exchange(
+        7, lambda k: (send_q.at[q_of(s_index(k + 1), zh)], recv_q.at[q], s_peer(k + 1, zh))
+    )
     recv_q[q] = send_q[q]
     for name in ("pick", "pick_m", "by_in", "by_out", "by_in_t", "spread", "spread_m"):
         loads[name].wait()
     args[4].wait()
     arrive(fifth)
+    arrive(fifth_far)
     wide_q[:, 0:10] = recv_q[...].astype(F32)
     halves = wide_q[...].reshape(256, 128).astype(BF16)
     chosen[...] = (mm(table("pick"), halves) * table("pick_m").astype(F32)).astype(BF16)
@@ -518,11 +521,10 @@
     back = mm(table("spread"), stack.astype(BF16))
     send_b[...] = back.reshape(8, 8, 128).astype(BF16)
 
-    def mode_home(k):
-        to = q_index(k + 1)
-        return send_b.at[(to // 4) * 2 + to % 2], recv_b.at[q], q_peer(k + 1)
-
-    sixth = exchange(15, mode_home)
+    sixth_far = exchange(
+        8, lambda k: (send_b.at[s_index(k)], recv_b.at[q], s_peer(k, 1 - zh))
+    )
+    sixth = exchange(7, lambda k: (send_b.at[s_index(k + 1)], recv_b.at[q], s_peer(k + 1)))
     recv_b[q] = send_b[s]
     out_copy_s = pltpu.make_async_copy(out_s, out_s_hbm, out_sem.at[4])
     out_copy_s.start()
@@ -531,6 +533,7 @@
     bypass_d = exchange(1, lambda k: (by_d.at[zh], by_d.at[zh], zh_peer()))
 
     arrive(sixth)
+    arrive(sixth_far)
     seventh = exchange(3, lambda k: (recv_b, recv_g.at[xx], x_peer(k + 1)))
     recv_g[xx] = recv_b[...]
     loads["row_i"].wait()
@@ -546,12 +549,21 @@
     arrive(eighth)
     turned = mm(table("reg_c"), rows_of(recv_l[...], 128))
     send_c[...] = turned.reshape(4, 3, 8, 128).astype(BF16)
+    halves = [pl.ds(0, 2), pl.ds(2, 2)]
+    across = (j + 4) % 8
+
+    def near(k):
+        return (j // 4) * 4 + (j + k) % 4
+
+    ninth_far = [
+        exchange(1, lambda k, h=h: (send_c.at[h], recv_c.at[j, h], (row, across))) for h in halves
+    ]
     ninth = exchange(
-        14,
+        6,
         lambda k: (
-            send_c.at[pl.ds((k // 7) * 2, 2)],
-            recv_c.at[j, pl.ds((k // 7) * 2, 2)],
-            col_peer(k % 7 + 1),
+            send_c.at[pl.ds((k // 3) * 2, 2)],
+            recv_c.at[j, pl.ds((k // 3) * 2, 2)],
+            (row, near(k % 3 + 1)),
         ),
     )
     recv_c[j] = send_c[...]
@@ -570,8 +582,18 @@
         out_copy(x).start()
         return carry
 
+    passed = []
     for half in range(2):
-        arrive(ninth, 7 * half, 7 * half + 7)
+        h = halves[half]
+        arrive(ninth_far[half])
+        passed.append(
+            exchange(
+                3, lambda k, h=h: (recv_c.at[across, h], recv_c.at[across, h], (row, near(k + 1)))
+            )
+        )
+    for half in range(2):
+        arrive(ninth, 3 * half, 3 * half + 3)
+        arrive(passed[half])
         lax.fori_loop(2 * half, 2 * half + 2, final, 0)
 
     for copy, count in exchanges:
@@ -584,6 +606,23 @@
     for x in range(4):
         out_copy(x).wait()
     out_copy_s.wait()
+
+
+def deliver(g, w, b, to_g, to_w, to_b, sem):
+    moves = [pltpu.make_async_copy(b, to_b, sem.at[6])]
+    for ri in range(2):
+        for half in range(2):
+            rows = slice(40 * half, 40 * half + 40)
+            moves.append(
+                pltpu.make_async_copy(w.at[ri, rows], to_w.at[ri, rows], sem.at[2 * ri + half])
+            )
+    for half in range(2):
+        rows = slice(2 * half, 2 * half + 2)
+        moves.append(pltpu.make_async_copy(g.at[rows], to_g.at[rows], sem.at[4 + half]))
+    for move in moves:
+        move.start()
+    for move in moves:
+        move.wait()
 
 
 N_COPIES = 14 + 7 + 3 + 7 + 1 + 7 + 7 + 3 + 15 + 15 + 3 + 7 + 14
@@ -640,7 +679,7 @@
         pltpu.SemaphoreType.DMA((N_COPIES,)),
         pltpu.SemaphoreType.DMA((N_COPIES,)),
     ]
-    grad_inputs, grad_weight, grad_bypass = pl.pallas_call(
+    results = pl.pallas_call(
         kernel,
         out_shape=(
             jax.ShapeDtypeStruct((4, 128, 256), BF16),
@@ -655,6 +694,16 @@
         ),
         name="fno_backward",
     )(inputs, preactivation, cotangent, weight, bypass, *[tables[k] for k in ORDER])
+    results = pl.pallas_call(
+        deliver,
+        out_shape=tuple(jax.ShapeDtypeStruct(o.shape, o.dtype) for o in results),
+        in_specs=[anywhere] * 3,
+        out_specs=(anywhere,) * 3,
+        scratch_shapes=[pltpu.SemaphoreType.DMA((7,))],
+        compiler_params=pltpu.CompilerParams(vmem_limit_bytes=62 * 1024 * 1024),
+        name="deliver",
+    )(*results)
+    grad_inputs, grad_weight, grad_bypass = results
     grad_spectral = grad_weight.reshape(2, 2, 5, 8, C * C).transpose(0, 1, 3, 2, 4)
     return (grad_inputs, grad_spectral, grad_bypass)
 

time: 89.4 us -> 114 us (1.28)
  Pallas kernels: 83.6 us -> 113 us
  local copies, waits for them, and re-layouts: 4.28 us -> 0 us
    pallas_call x0 -> x1, Pallas kernels: none -> 29.5 us  [local(): pl.pallas_call(deliver, out_shape=tuple((jax.ShapeDtypeStruct(o.shape, o....]
    unnamed x5 -> x0, local copies, waits for them, and re-layouts: 4.28 us -> none
where the time goes in v4:
time: 114 us
  Pallas kernels  113 us (99%)
    pallas_call x1, Pallas kernels, local(): pl.pallas_call(kernel, out_shape=(jax.ShapeDtypeStruct((4, 128, 256), BF1...  83.8 us
    pallas_call x1, Pallas kernels, local(): pl.pallas_call(deliver, out_shape=tuple((jax.ShapeDtypeStruct(o.shape, o....  29.5 us

profile of v4, /device:TPU:1, one launch (start us, length us, event | category | flops | bytes accessed | tf_op | source)
XLA Modules:
  0.0 113.9 jit_solution(5468852235924222932)
XLA Ops:
  0.6 83.8 %fno_backward.1 = (bf16[4,128,256]{2,1,0:T(8,128)(2,1)}, f32[2,80,1024]{2,1,0:T(8,128)}, f32[32,32]{1,0:T(8,128)}) custom-call(bf16[4,128,256]{2,1,0:T(8,128)(2,1)} %inp_hbm.1, bf16[4,128,256]{2,1,0:T(8,128)(2,1)} %pre_hbm.1, bf16[4,128,256]{2,1,0:T(8,128)(2,1)} %cot_hbm.1, bf16[2,80,1024]{2,1,0:T(8,128)(2,1)} %bitcast.6, bf16[32,32]{1,0:T(8,128)(2,1)} %byp_hbm.1, ...), custom_call_target="tpu_custom_call" | custom-call | tf_op jit(solution)/shard_map/fno_backward/pallas_call | solution.py:682
  84.5 29.5 %deliver.1 = (bf16[4,128,256]{2,1,0:T(8,128)(2,1)}, f32[2,80,1024]{2,1,0:T(8,128)}, f32[32,32]{1,0:T(8,128)}) custom-call(bf16[4,128,256]{2,1,0:T(8,128)(2,1)} %get-tuple-element.9.g, f32[2,80,1024]{2,1,0:T(8,128)} %get-tuple-element.10.w, f32[32,32]{1,0:T(8,128)} %get-tuple-element.11.b), custom_call_target="tpu_custom_call" | custom-call | tf_op jit(solution)/shard_map/deliver/pallas_call | solution.py:697

commit v5 on v4

--- a/solution.py
+++ b/solution.py
@@ -90,16 +90,15 @@
     cos, sin = turns(freq, np.arange(NX), NX)
     cos = cos.reshape(4, 16, 2, 4, 4, 2, 2, 4)
     sin = sin.reshape(4, 16, 2, 4, 4, 2, 2, 4)
-    forward = np.zeros((4, 2, 4, 16, 2, 2, 4, 2, 2, 4))
+    forward = np.zeros((4, 4, 16, 2, 2, 4, 2, 2, 2, 4))
     for xx in range(4):
-        for zh in range(2):
-            c = cos[:, :, :, xx, :, zh]
-            s = sin[:, :, :, xx, :, zh]
-            forward[xx, zh, :, :, :, 0, :, :, 0, :] = c
-            forward[xx, zh, :, :, :, 0, :, :, 1, :] = s
-            forward[xx, zh, :, :, :, 1, :, :, 1, :] = c
-            forward[xx, zh, :, :, :, 1, :, :, 0, :] = -s
-    forward = forward.reshape(8, 256, 64)
+        c = cos[:, :, :, xx].transpose(0, 1, 2, 3, 5, 4, 6)
+        s = sin[:, :, :, xx].transpose(0, 1, 2, 3, 5, 4, 6)
+        forward[xx, :, :, :, 0, :, :, :, 0, :] = c
+        forward[xx, :, :, :, 0, :, :, :, 1, :] = s
+        forward[xx, :, :, :, 1, :, :, :, 1, :] = c
+        forward[xx, :, :, :, 1, :, :, :, 0, :] = -s
+    forward = forward.reshape(4, 256, 128)
     deal = np.zeros((16, 16, 3, 16, 2, 2))
     for q in range(16):
         for e in range(2):
@@ -107,17 +106,16 @@
                 for slab in range(2):
                     deal[q, slab * 4 + e * 2 + ab, slab, q, e, ab] = 1.0
             deal[q, 8 + e, 2, q, e, 0] = 1.0
-    inverse = np.zeros((4, 2, 4, 2, 2, 2, 4, 4, 16, 2, 2, 2))
+    inverse = np.zeros((4, 4, 2, 2, 2, 2, 4, 4, 16, 2, 2, 2))
     for xx in range(4):
-        for zh in range(2):
-            for slab in range(2):
-                c = cos[:, :, :, xx, :, zh].transpose(3, 4, 5, 0, 1, 2)
-                s = sin[:, :, :, xx, :, zh].transpose(3, 4, 5, 0, 1, 2)
-                inverse[xx, zh, :, :, slab, 0, :, :, :, slab, :, 0] = c
-                inverse[xx, zh, :, :, slab, 0, :, :, :, slab, :, 1] = -s
-                inverse[xx, zh, :, :, slab, 1, :, :, :, slab, :, 1] = c
-                inverse[xx, zh, :, :, slab, 1, :, :, :, slab, :, 0] = s
-    return forward, inverse.reshape(8, 128, 512), deal.reshape(256, 192)
+        for slab in range(2):
+            c = cos[:, :, :, xx].transpose(3, 5, 4, 6, 0, 1, 2)
+            s = sin[:, :, :, xx].transpose(3, 5, 4, 6, 0, 1, 2)
+            inverse[xx, :, :, :, slab, 0, :, :, :, slab, :, 0] = c
+            inverse[xx, :, :, :, slab, 0, :, :, :, slab, :, 1] = -s
+            inverse[xx, :, :, :, slab, 1, :, :, :, slab, :, 1] = c
+            inverse[xx, :, :, :, slab, 1, :, :, :, slab, :, 0] = s
+    return forward, inverse.reshape(4, 256, 512), deal.reshape(256, 192)
 
 
 def mixing_tables():
@@ -266,7 +264,7 @@
         inp, pre, cot, spec, byp, out_g, out_s, arg_sem, out_sem,
         grad, plus, pieces, recv_col, send_s, recv_s, send_x, recv_x, send_q, recv_q,
         send_b, recv_b, recv_g, send_l, recv_l, send_c, recv_c,
-        by_sum, wide_q, by_a, by_b, by_c, by_d, by_e,
+        total, by_sum, wide_q, by_a, by_b, by_c, by_e,
         lined, high, product, blocks, chosen, repeated,
         table_sem, send_sem, recv_sem,
     ) = refs[2 * n + 3 :]
@@ -280,8 +278,19 @@
     core = q % 2
     s = yy * 2 + core
 
-    def col_peer(k):
-        return row, (j + k) % 8
+    z = zh * 8 + j
+
+    def ring_step(k):
+        d = 4 - (k + 1) // 2
+        odd = k % 2
+        return odd * d + (1 - odd) * (16 - d) + 8 * core * (1 - (k + 6) // 7)
+
+    def z_index(o):
+        return (z + o) % 16
+
+    def z_peer(o):
+        other = z_index(o)
+        return xx * 16 + yy * 4 + (other // 8) * 2 + core, other % 8
 
     def s_index(k):
         return (s + k) % 8
@@ -292,23 +301,21 @@
     def s_peer(k, half=zh):
         return xx * 16 + q_of(s_index(k), half), j
 
-    def zh_peer():
-        return s_peer(0, 1 - zh)
 
     def x_peer(k):
         return ((xx + k) % 4) * 16 + q, j
 
     barrier = pltpu.get_barrier_semaphore()
     everyone = (
-        [col_peer(k) for k in range(1, 8)]
+        [z_peer(o) for o in range(1, 16)]
         + [s_peer(k) for k in range(1, 8)]
-        + [s_peer(k, 1 - zh) for k in range(8)]
+        + [s_peer(k, 1 - zh) for k in range(1, 8)]
         + [x_peer(k) for k in range(1, 4)]
     )
     for peer in everyone:
         pl.semaphore_signal(barrier, inc=1, device_id=peer, device_id_type=MESH)
 
-    index_of = {"col_f": j, "col_i": j, "row_f": xx * 2 + zh, "row_i": xx * 2 + zh}
+    index_of = {"col_f": j, "col_i": j, "row_f": xx, "row_i": xx}
     loads = {}
 
     def load(name):
@@ -391,9 +398,9 @@
     first_in = exchange(
         7,
         lambda k: (
-            pieces.at[(j + k + 1) % 8, 0:2],
+            pieces.at[z_index(ring_step(k)) % 8, 0:2],
             recv_col.at[k, 0:2],
-            col_peer(k + 1),
+            z_peer(ring_step(k)),
         ),
     )
     args[1].wait()
@@ -419,9 +426,9 @@
     first_grad = exchange(
         7,
         lambda k: (
-            pieces.at[(j + k + 1) % 8, 2:5],
+            pieces.at[z_index(ring_step(k)) % 8, 2:5],
             recv_col.at[k, 2:5],
-            col_peer(k + 1),
+            z_peer(ring_step(k)),
         ),
     )
 
@@ -449,11 +456,18 @@
         loads[name].wait()
     arrive(first_in)
     arrive(first_grad)
-    total = pieces[j].astype(F32).reshape(160, 128)
-    for k in range(7):
-        total += recv_col[k].astype(F32).reshape(160, 128)
-    grouped = regroup_forward(total, table("reg_a"), table("reg_b"), table("reg_l"))
-    send_s[...] = grouped.reshape(8, 3, 8, 128).astype(BF16)
+    total[zh] = pieces[j].astype(F32).reshape(160, 128)
+    total[1 - zh] = jnp.zeros((160, 128), F32)
+
+    def add_terms(k, carry):
+        half = z_index(32 - ring_step(k)) // 8
+        total[half] += recv_col[k].astype(F32).reshape(160, 128)
+        return carry
+
+    lax.fori_loop(0, 7, add_terms, 0)
+    for half in range(2):
+        grouped = regroup_forward(total[half], table("reg_a"), table("reg_b"), table("reg_l"))
+        send_s[:, half] = grouped.reshape(8, 3, 8, 128).astype(BF16)
     recv_s[s] = send_s[s]
     second = exchange(7, lambda k: (send_s.at[s_index(k + 1)], recv_s.at[s], s_peer(k + 1)))
 
@@ -466,14 +480,14 @@
     loads["row_f"].wait()
     loads["deal"].wait()
     arrive(second)
-    rows = jnp.concatenate([rows_of(recv_s[:, slab], 64) for slab in range(3)], axis=1)
+    rows = jnp.concatenate([rows_of(recv_s[:, :, slab], 128) for slab in range(3)], axis=1)
     send_x[...] = mm(table("row_f"), rows).reshape(4, 64, 384).astype(BF16)
     fourth = exchange(
         3, lambda k: (send_x.at[(xx + k + 1) % 4], recv_x.at[k], x_peer(k + 1))
     )
     arrive(bypass_b)
-    by_c[j] = by_b[...].sum(0)
-    bypass_c = exchange(7, lambda k: (by_c.at[j], by_c.at[j], col_peer(k + 1)))
+    by_c[z] = by_b[...].sum(0)
+    bypass_c = exchange(15, lambda k: (by_c.at[z], by_c.at[z], z_peer(k + 1)))
     arrive(fourth)
     summed = send_x[xx].astype(F32)
     for k in range(3):
@@ -528,9 +542,6 @@
     recv_b[q] = send_b[s]
     out_copy_s = pltpu.make_async_copy(out_s, out_s_hbm, out_sem.at[4])
     out_copy_s.start()
-    arrive(bypass_c)
-    by_d[zh] = by_c[...].sum(0)
-    bypass_d = exchange(1, lambda k: (by_d.at[zh], by_d.at[zh], zh_peer()))
 
     arrive(sixth)
     arrive(sixth_far)
@@ -540,33 +551,25 @@
     loads["reg_c"].wait()
     arrive(seventh)
     lines = mm(table("row_i"), rows_of(recv_g[...], 512))
-    send_l[...] = lines.reshape(8, 16, 128).astype(BF16)
+    send_l[...] = lines.reshape(8, 2, 16, 128).astype(BF16)
     eighth = exchange(7, lambda k: (send_l.at[s_index(k + 1)], recv_l.at[s], s_peer(k + 1)))
     recv_l[s] = send_l[s]
-    arrive(bypass_d)
-    by_e[s] = by_d[...].sum(0)
+    arrive(bypass_c)
+    by_e[s] = by_c[...].sum(0)
     bypass_e = exchange(7, lambda k: (by_e.at[s], by_e.at[s], s_peer(k + 1)))
     arrive(eighth)
-    turned = mm(table("reg_c"), rows_of(recv_l[...], 128))
-    send_c[...] = turned.reshape(4, 3, 8, 128).astype(BF16)
-    halves = [pl.ds(0, 2), pl.ds(2, 2)]
-    across = (j + 4) % 8
-
-    def near(k):
-        return (j // 4) * 4 + (j + k) % 4
-
-    ninth_far = [
-        exchange(1, lambda k, h=h: (send_c.at[h], recv_c.at[j, h], (row, across))) for h in halves
-    ]
+    for half in range(2):
+        turned = mm(table("reg_c"), rows_of(recv_l[:, half], 128))
+        send_c[half] = turned.reshape(4, 3, 8, 128).astype(BF16)
     ninth = exchange(
-        6,
+        7,
         lambda k: (
-            send_c.at[pl.ds((k // 3) * 2, 2)],
-            recv_c.at[j, pl.ds((k // 3) * 2, 2)],
-            (row, near(k % 3 + 1)),
+            send_c.at[z_index(ring_step(k)) // 8],
+            recv_c.at[j],
+            z_peer(ring_step(k)),
         ),
     )
-    recv_c[j] = send_c[...]
+    recv_c[j] = send_c[zh]
     loads["time_i"].wait()
     loads["col_i"].wait()
     arrive(bypass_e)
@@ -582,19 +585,8 @@
         out_copy(x).start()
         return carry
 
-    passed = []
-    for half in range(2):
-        h = halves[half]
-        arrive(ninth_far[half])
-        passed.append(
-            exchange(
-                3, lambda k, h=h: (recv_c.at[across, h], recv_c.at[across, h], (row, near(k + 1)))
-            )
-        )
-    for half in range(2):
-        arrive(ninth, 3 * half, 3 * half + 3)
-        arrive(passed[half])
-        lax.fori_loop(2 * half, 2 * half + 2, final, 0)
+    arrive(ninth)
+    lax.fori_loop(0, 4, final, 0)
 
     for copy, count in exchanges:
 
@@ -608,24 +600,27 @@
     out_copy_s.wait()
 
 
-def deliver(g, w, b, to_g, to_w, to_b, sem):
-    moves = [pltpu.make_async_copy(b, to_b, sem.at[6])]
-    for ri in range(2):
-        for half in range(2):
-            rows = slice(40 * half, 40 * half + 40)
-            moves.append(
-                pltpu.make_async_copy(w.at[ri, rows], to_w.at[ri, rows], sem.at[2 * ri + half])
-            )
-    for half in range(2):
-        rows = slice(2 * half, 2 * half + 2)
-        moves.append(pltpu.make_async_copy(g.at[rows], to_g.at[rows], sem.at[4 + half]))
-    for move in moves:
-        move.start()
-    for move in moves:
-        move.wait()
-
-
-N_COPIES = 14 + 7 + 3 + 7 + 1 + 7 + 7 + 3 + 15 + 15 + 3 + 7 + 14
+def deliver(g, w, b, to_g, to_w, to_b, held_g, held_w, held_b, sem_in, sem_out):
+    pieces = [(b, held_b, to_b)]
+    pieces += [(w.at[i, h], held_w.at[i, h], to_w.at[i, h]) for i in range(2) for h in HALVES]
+    pieces += [(g.at[i], held_g.at[i], to_g.at[i]) for i in range(4)]
+    fetch = [
+        pltpu.make_async_copy(p[0], p[1], sem_in.at[i]) for i, p in enumerate(pieces)
+    ]
+    store = [
+        pltpu.make_async_copy(p[1], p[2], sem_out.at[i]) for i, p in enumerate(pieces)
+    ]
+    for copy in fetch:
+        copy.start()
+    for i in range(len(pieces)):
+        fetch[i].wait()
+        store[i].start()
+    for copy in store:
+        copy.wait()
+
+
+HALVES = (slice(0, 40), slice(40, 80))
+N_COPIES = 14 + 7 + 3 + 15 + 7 + 7 + 3 + 15 + 15 + 3 + 7 + 7
 
 
 def local(inputs, preactivation, cotangent, spectral, bypass, tables):
@@ -649,8 +644,8 @@
         pltpu.VMEM((4, 128, 256), F32),
         pltpu.VMEM((8, 5, 4, 8, 128), BF16),
         pltpu.VMEM((7, 5, 4, 8, 128), BF16),
-        pltpu.VMEM((8, 3, 8, 128), BF16),
-        pltpu.VMEM((8, 3, 8, 128), BF16),
+        pltpu.VMEM((8, 2, 3, 8, 128), BF16),
+        pltpu.VMEM((8, 2, 3, 8, 128), BF16),
         pltpu.VMEM((4, 64, 384), BF16),
         pltpu.VMEM((3, 64, 384), BF16),
         pltpu.VMEM((16, 10, 128), BF16),
@@ -658,16 +653,16 @@
         pltpu.VMEM((8, 8, 128), BF16),
         pltpu.VMEM((16, 8, 128), BF16),
         pltpu.VMEM((4, 16, 8, 128), BF16),
-        pltpu.VMEM((8, 16, 128), BF16),
-        pltpu.VMEM((8, 16, 128), BF16),
-        pltpu.VMEM((4, 3, 8, 128), BF16),
+        pltpu.VMEM((8, 2, 16, 128), BF16),
+        pltpu.VMEM((8, 2, 16, 128), BF16),
+        pltpu.VMEM((2, 4, 3, 8, 128), BF16),
         pltpu.VMEM((8, 4, 3, 8, 128), BF16),
+        pltpu.VMEM((2, 160, 128), F32),
         pltpu.VMEM((8, 128), F32),
         pltpu.VMEM((16, 16, 128), F32),
         pltpu.VMEM((8, 8, 128), F32),
         pltpu.VMEM((4, 1, 128), F32),
-        pltpu.VMEM((8, 1, 128), F32),
-        pltpu.VMEM((2, 1, 128), F32),
+        pltpu.VMEM((16, 1, 128), F32),
         pltpu.VMEM((8, 1, 128), F32),
         pltpu.VMEM((4, 64, 512), BF16),
         pltpu.VMEM((256, 128), F32),
@@ -699,7 +694,8 @@
         out_shape=tuple(jax.ShapeDtypeStruct(o.shape, o.dtype) for o in results),
         in_specs=[anywhere] * 3,
         out_specs=(anywhere,) * 3,
-        scratch_shapes=[pltpu.SemaphoreType.DMA((7,))],
+        scratch_shapes=[pltpu.VMEM(o.shape, o.dtype) for o in results]
+        + [pltpu.SemaphoreType.DMA((9,)), pltpu.SemaphoreType.DMA((9,))],
         compiler_params=pltpu.CompilerParams(vmem_limit_bytes=62 * 1024 * 1024),
         name="deliver",
     )(*results)

time: 114 us -> 79.6 us (0.70)
  Pallas kernels: 113 us -> 78.7 us
    pallas_call x1, Pallas kernels: 29.5 us -> 2.07 us  [local(): pl.pallas_call(deliver, out_shape=tuple((jax.ShapeDtypeStruct(o.shape, o....]
    pallas_call x1, Pallas kernels: 83.8 us -> 76.6 us  [local(): pl.pallas_call(kernel, out_shape=(jax.ShapeDtypeStruct((4, 128, 256), BF1...]
where the time goes in v5:
time: 79.6 us; the launch traced here: 79.4 us
  Pallas kernels  78.7 us (99%)
    pallas_call x1, Pallas kernels, local(): pl.pallas_call(kernel, out_shape=(jax.ShapeDtypeStruct((4, 128, 256), BF1...  76.6 us
    pallas_call x1, Pallas kernels, local(): pl.pallas_call(deliver, out_shape=tuple((jax.ShapeDtypeStruct(o.shape, o....  2.07 us

profile of v5, /device:TPU:1, one launch (start us, length us, event | category | flops | bytes accessed | tf_op | source)
XLA Modules:
  0.0 79.4 jit_solution(3401422219869330898)
XLA Ops:
  0.6 76.6 %fno_backward.1 = (bf16[4,128,256]{2,1,0:T(8,128)(2,1)}, f32[2,80,1024]{2,1,0:T(8,128)}, f32[32,32]{1,0:T(8,128)}) custom-call(bf16[4,128,256]{2,1,0:T(8,128)(2,1)} %inp_hbm.1, bf16[4,128,256]{2,1,0:T(8,128)(2,1)} %pre_hbm.1, bf16[4,128,256]{2,1,0:T(8,128)(2,1)} %cot_hbm.1, bf16[2,80,1024]{2,1,0:T(8,128)(2,1)} %bitcast.6, bf16[32,32]{1,0:T(8,128)(2,1)} %byp_hbm.1, ...), custom_call_target="tpu_custom_call" | custom-call | tf_op jit(solution)/shard_map/fno_backward/pallas_call | solution.py:677
  77.3 2.1 %deliver.1 = (bf16[4,128,256]{2,1,0:T(8,128)(2,1)}, f32[2,80,1024]{2,1,0:T(8,128)}, f32[32,32]{1,0:T(8,128)}) custom-call(bf16[4,128,256]{2,1,0:T(8,128)(2,1)} %get-tuple-element.9.g, f32[2,80,1024]{2,1,0:T(8,128)} %get-tuple-element.10.w, f32[32,32]{1,0:T(8,128)} %get-tuple-element.11.b), custom_call_target="tpu_custom_call" | custom-call | tf_op jit(solution)/shard_map/deliver/pallas_call | solution.py:692

commit v6 on v5

--- a/solution.py
+++ b/solution.py
@@ -72,14 +72,9 @@
             swapped[k, 2, 1, x, 4, x, k] = 1.0
             for tile in range(3):
                 back[x, tile, k, k, tile // 2, tile % 2, x] = 1.0
-    lanes = np.zeros((2, 2, C, 2, 2, C))
-    for f in range(2):
-        lanes[f, 1, :, f, 0, :] = np.eye(C)
-        lanes[f, 0, :, f, 1, :] = -np.eye(C)
     return (
         direct.reshape(192, 160),
-        swapped.reshape(192, 160),
-        lanes.reshape(128, 128),
+        swapped.reshape(192, 160)[:, 128:],
         back.reshape(96, 128),
     )
 
@@ -166,7 +161,7 @@
     t = {}
     t["col_f"], t["col_i"] = column_tables()
     t["time_f"], t["time_i"] = time_tables()
-    t["reg_a"], t["reg_b"], t["reg_l"], t["reg_c"] = regroup_tables()
+    t["reg_a"], t["reg_b"], t["reg_c"] = regroup_tables()
     t["row_f"], t["row_i"], t["deal"] = row_tables()
     t["pick"], t["pick_m"], t["by_in"], t["by_out"], t["by_in_t"], t["spread"], t["spread_m"] = (
         mixing_tables()
@@ -176,7 +171,7 @@
 
 PICKED = ("col_f", "col_i", "row_f", "row_i")
 ORDER = (
-    "col_f", "time_f", "reg_a", "reg_b", "reg_l", "row_f", "deal", "pick", "pick_m", "by_in",
+    "col_f", "time_f", "reg_a", "reg_b", "row_f", "deal", "pick", "pick_m", "by_in",
     "by_out", "by_in_t", "spread", "spread_m", "row_i", "reg_c", "time_i", "col_i",
 )
 
@@ -239,10 +234,13 @@
     return jnp.where(row // C == lane // C, full, 0.0).astype(BF16)
 
 
-def regroup_forward(total, reg_a, reg_b, reg_l):
+def regroup_forward(total, reg_a, reg_b):
     rows = total.astype(BF16)
-    turned = mm(rows, reg_l).astype(BF16)
-    return mm(reg_a, rows) + mm(reg_b, turned)
+    last = total[128:160]
+    lane = lax.broadcasted_iota(jnp.int32, (C, 128), 1)
+    real = (lane // C) % 2 == 0
+    turned = jnp.where(real, pltpu.roll(last, 96, 1), -pltpu.roll(last, 32, 1))
+    return mm(reg_a, rows) + mm(reg_b, turned.astype(BF16))
 
 
 def final_rows(low_re, low_im, high, time_i, col_i):
@@ -281,35 +279,34 @@
     z = zh * 8 + j
 
     def ring_step(k):
-        d = 4 - (k + 1) // 2
-        odd = k % 2
-        return odd * d + (1 - odd) * (16 - d) + 8 * core * (1 - (k + 6) // 7)
+        d = 4 - lax.div(k + 1, 2)
+        odd = lax.rem(k, 2)
+        return odd * d + (1 - odd) * (16 - d) + 8 * core * (1 - lax.div(k + 6, 7))
 
     def z_index(o):
-        return (z + o) % 16
+        return lax.rem(z + o, 16)
 
     def z_peer(o):
         other = z_index(o)
-        return xx * 16 + yy * 4 + (other // 8) * 2 + core, other % 8
+        return xx * 16 + yy * 4 + lax.div(other, 8) * 2 + core, lax.rem(other, 8)
 
     def s_index(k):
-        return (s + k) % 8
+        return lax.rem(s + k, 8)
 
     def q_of(other, half):
-        return (other // 2) * 4 + half * 2 + other % 2
+        return lax.div(other, 2) * 4 + half * 2 + lax.rem(other, 2)
 
     def s_peer(k, half=zh):
         return xx * 16 + q_of(s_index(k), half), j
 
 
     def x_peer(k):
-        return ((xx + k) % 4) * 16 + q, j
+        return lax.rem(xx + k, 4) * 16 + q, j
 
     barrier = pltpu.get_barrier_semaphore()
     everyone = (
-        [z_peer(o) for o in range(1, 16)]
+        [z_peer(o) for o in (1, 2, 3, 4, 12, 13, 14, 15)]
         + [s_peer(k) for k in range(1, 8)]
-        + [s_peer(k, 1 - zh) for k in range(1, 8)]
         + [x_peer(k) for k in range(1, 4)]
     )
     for peer in everyone:
@@ -377,6 +374,16 @@
 
         lax.fori_loop(first, count if last is None else last, wait, 0)
 
+    def drain():
+        for copy, count in exchanges:
+
+            def left(k, carry, copy=copy):
+                copy(k).wait_send()
+                return carry
+
+            lax.fori_loop(0, count, left, 0)
+        exchanges.clear()
+
     loads["col_f"].wait()
     args[0].wait()
 
@@ -398,7 +405,7 @@
     first_in = exchange(
         7,
         lambda k: (
-            pieces.at[z_index(ring_step(k)) % 8, 0:2],
+            pieces.at[lax.rem(z_index(ring_step(k)), 8), 0:2],
             recv_col.at[k, 0:2],
             z_peer(ring_step(k)),
         ),
@@ -426,7 +433,7 @@
     first_grad = exchange(
         7,
         lambda k: (
-            pieces.at[z_index(ring_step(k)) % 8, 2:5],
+            pieces.at[lax.rem(z_index(ring_step(k)), 8), 2:5],
             recv_col.at[k, 2:5],
             z_peer(ring_step(k)),
         ),
@@ -452,7 +459,7 @@
 
     lax.fori_loop(0, 4, pointwise, 0)
 
-    for name in ("reg_a", "reg_b", "reg_l"):
+    for name in ("reg_a", "reg_b"):
         loads[name].wait()
     arrive(first_in)
     arrive(first_grad)
@@ -460,13 +467,13 @@
     total[1 - zh] = jnp.zeros((160, 128), F32)
 
     def add_terms(k, carry):
-        half = z_index(32 - ring_step(k)) // 8
+        half = lax.div(z_index(32 - ring_step(k)), 8)
         total[half] += recv_col[k].astype(F32).reshape(160, 128)
         return carry
 
     lax.fori_loop(0, 7, add_terms, 0)
     for half in range(2):
-        grouped = regroup_forward(total[half], table("reg_a"), table("reg_b"), table("reg_l"))
+        grouped = regroup_forward(total[half], table("reg_a"), table("reg_b"))
         send_s[:, half] = grouped.reshape(8, 3, 8, 128).astype(BF16)
     recv_s[s] = send_s[s]
     second = exchange(7, lambda k: (send_s.at[s_index(k + 1)], recv_s.at[s], s_peer(k + 1)))
@@ -483,11 +490,8 @@
     rows = jnp.concatenate([rows_of(recv_s[:, :, slab], 128) for slab in range(3)], axis=1)
     send_x[...] = mm(table("row_f"), rows).reshape(4, 64, 384).astype(BF16)
     fourth = exchange(
-        3, lambda k: (send_x.at[(xx + k + 1) % 4], recv_x.at[k], x_peer(k + 1))
-    )
-    arrive(bypass_b)
-    by_c[z] = by_b[...].sum(0)
-    bypass_c = exchange(15, lambda k: (by_c.at[z], by_c.at[z], z_peer(k + 1)))
+        3, lambda k: (send_x.at[lax.rem(xx + k + 1, 4)], recv_x.at[k], x_peer(k + 1))
+    )
     arrive(fourth)
     summed = send_x[xx].astype(F32)
     for k in range(3):
@@ -497,6 +501,8 @@
     dealt = mm(table("deal"), summed).reshape(16, 16, 128)
     send_q[...] = dealt[:, 0:10].astype(BF16)
 
+    earlier = list(exchanges)
+    exchanges.clear()
     fifth_far = exchange(
         8, lambda k: (send_q.at[q_of(s_index(k), 1 - zh)], recv_q.at[q], s_peer(k, 1 - zh))
     )
@@ -504,6 +510,12 @@
         7, lambda k: (send_q.at[q_of(s_index(k + 1), zh)], recv_q.at[q], s_peer(k + 1, zh))
     )
     recv_q[q] = send_q[q]
+    arrive(bypass_b)
+    by_c[z] = by_b[...].sum(0)
+    bypass_c = exchange(15, lambda k: (by_c.at[z], by_c.at[z], z_peer(k + 1)))
+    later = list(exchanges)
+    exchanges[:] = earlier
+    drain()
     for name in ("pick", "pick_m", "by_in", "by_out", "by_in_t", "spread", "spread_m"):
         loads[name].wait()
     args[4].wait()
@@ -540,6 +552,9 @@
     )
     sixth = exchange(7, lambda k: (send_b.at[s_index(k + 1)], recv_b.at[q], s_peer(k + 1)))
     recv_b[q] = send_b[s]
+    latest = exchanges[:]
+    exchanges[:] = later
+    drain()
     out_copy_s = pltpu.make_async_copy(out_s, out_s_hbm, out_sem.at[4])
     out_copy_s.start()
 
@@ -564,12 +579,16 @@
     ninth = exchange(
         7,
         lambda k: (
-            send_c.at[z_index(ring_step(k)) // 8],
+            send_c.at[lax.div(z_index(ring_step(k)), 8)],
             recv_c.at[j],
             z_peer(ring_step(k)),
         ),
     )
     recv_c[j] = send_c[zh]
+    last = exchanges[:]
+    exchanges[:] = latest + last[:-1]
+    drain()
+    exchanges[:] = last[-1:]
     loads["time_i"].wait()
     loads["col_i"].wait()
     arrive(bypass_e)
@@ -588,13 +607,7 @@
     arrive(ninth)
     lax.fori_loop(0, 4, final, 0)
 
-    for copy, count in exchanges:
-
-        def drain(k, carry, copy=copy):
-            copy(k).wait_send()
-            return carry
-
-        lax.fori_loop(0, count, drain, 0)
+    drain()
     for x in range(4):
         out_copy(x).wait()
     out_copy_s.wait()

time: 79.6 us -> 73.5 us (0.923)
  Pallas kernels: 78.7 us -> 72.6 us
    pallas_call x1, Pallas kernels: 76.6 us -> 70.5 us  [local(): pl.pallas_call(kernel, out_shape=(jax.ShapeDtypeStruct((4, 128, 256), BF1...]
where the time goes in v6:
time: 73.5 us; the launch traced here: 73.3 us
  Pallas kernels  72.6 us (99%)
    pallas_call x1, Pallas kernels, local(): pl.pallas_call(kernel, out_shape=(jax.ShapeDtypeStruct((4, 128, 256), BF1...  70.5 us
    pallas_call x1, Pallas kernels, local(): pl.pallas_call(deliver, out_shape=tuple((jax.ShapeDtypeStruct(o.shape, o....  2.07 us

profile of v6, /device:TPU:1, one launch (start us, length us, event | category | flops | bytes accessed | tf_op | source)
XLA Modules:
  0.0 73.3 jit_solution(400067931088084438)
XLA Ops:
  0.6 70.5 %fno_backward.1 = (bf16[4,128,256]{2,1,0:T(8,128)(2,1)}, f32[2,80,1024]{2,1,0:T(8,128)}, f32[32,32]{1,0:T(8,128)}) custom-call(bf16[4,128,256]{2,1,0:T(8,128)(2,1)} %inp_hbm.1, bf16[4,128,256]{2,1,0:T(8,128)(2,1)} %pre_hbm.1, bf16[4,128,256]{2,1,0:T(8,128)(2,1)} %cot_hbm.1, bf16[2,80,1024]{2,1,0:T(8,128)(2,1)} %bitcast.6, bf16[32,32]{1,0:T(8,128)(2,1)} %byp_hbm.1, ...), custom_call_target="tpu_custom_call" | custom-call | tf_op jit(solution)/shard_map/fno_backward/pallas_call | solution.py:690
  71.2 2.1 %deliver.1 = (bf16[4,128,256]{2,1,0:T(8,128)(2,1)}, f32[2,80,1024]{2,1,0:T(8,128)}, f32[32,32]{1,0:T(8,128)}) custom-call(bf16[4,128,256]{2,1,0:T(8,128)(2,1)} %get-tuple-element.9.g, f32[2,80,1024]{2,1,0:T(8,128)} %get-tuple-element.10.w, f32[32,32]{1,0:T(8,128)} %get-tuple-element.11.b), custom_call_target="tpu_custom_call" | custom-call | tf_op jit(solution)/shard_map/deliver/pallas_call | solution.py:705

commit v7 on v6

--- a/solution.py
+++ b/solution.py
@@ -303,6 +303,9 @@
     def x_peer(k):
         return lax.rem(xx + k, 4) * 16 + q, j
 
+    def far(k):
+        return lax.rem(k + 1, 3) + 1
+
     barrier = pltpu.get_barrier_semaphore()
     everyone = (
         [z_peer(o) for o in (1, 2, 3, 4, 12, 13, 14, 15)]
@@ -490,7 +493,7 @@
     rows = jnp.concatenate([rows_of(recv_s[:, :, slab], 128) for slab in range(3)], axis=1)
     send_x[...] = mm(table("row_f"), rows).reshape(4, 64, 384).astype(BF16)
     fourth = exchange(
-        3, lambda k: (send_x.at[lax.rem(xx + k + 1, 4)], recv_x.at[k], x_peer(k + 1))
+        3, lambda k: (send_x.at[lax.rem(xx + far(k), 4)], recv_x.at[k], x_peer(far(k)))
     )
     arrive(fourth)
     summed = send_x[xx].astype(F32)
@@ -560,7 +563,7 @@
 
     arrive(sixth)
     arrive(sixth_far)
-    seventh = exchange(3, lambda k: (recv_b, recv_g.at[xx], x_peer(k + 1)))
+    seventh = exchange(3, lambda k: (recv_b, recv_g.at[xx], x_peer(far(k))))
     recv_g[xx] = recv_b[...]
     loads["row_i"].wait()
     loads["reg_c"].wait()

time: 73.5 us -> 73.4 us (level)
  no operation moved by 1% of the time
where the time goes in v7:
time: 73.4 us; the launch traced here: 73.2 us
  Pallas kernels  72.6 us (99%)
    pallas_call x1, Pallas kernels, local(): pl.pallas_call(kernel, out_shape=(jax.ShapeDtypeStruct((4, 128, 256), BF1...  70.5 us
    pallas_call x1, Pallas kernels, local(): pl.pallas_call(deliver, out_shape=tuple((jax.ShapeDtypeStruct(o.shape, o....  2.07 us

profile of v7, /device:TPU:1, one launch (start us, length us, event | category | flops | bytes accessed | tf_op | source)
XLA Modules:
  0.0 73.2 jit_solution(283396212015269642)
XLA Ops:
  0.6 70.5 %fno_backward.1 = (bf16[4,128,256]{2,1,0:T(8,128)(2,1)}, f32[2,80,1024]{2,1,0:T(8,128)}, f32[32,32]{1,0:T(8,128)}) custom-call(bf16[4,128,256]{2,1,0:T(8,128)(2,1)} %inp_hbm.1, bf16[4,128,256]{2,1,0:T(8,128)(2,1)} %pre_hbm.1, bf16[4,128,256]{2,1,0:T(8,128)(2,1)} %cot_hbm.1, bf16[2,80,1024]{2,1,0:T(8,128)(2,1)} %bitcast.6, bf16[32,32]{1,0:T(8,128)(2,1)} %byp_hbm.1, ...), custom_call_target="tpu_custom_call" | custom-call | tf_op jit(solution)/shard_map/fno_backward/pallas_call | solution.py:693
  71.1 2.1 %deliver.1 = (bf16[4,128,256]{2,1,0:T(8,128)(2,1)}, f32[2,80,1024]{2,1,0:T(8,128)}, f32[32,32]{1,0:T(8,128)}) custom-call(bf16[4,128,256]{2,1,0:T(8,128)(2,1)} %get-tuple-element.9.g, f32[2,80,1024]{2,1,0:T(8,128)} %get-tuple-element.10.w, f32[32,32]{1,0:T(8,128)} %get-tuple-element.11.b), custom_call_target="tpu_custom_call" | custom-call | tf_op jit(solution)/shard_map/deliver/pallas_call | solution.py:708
